TPU v7x, 1024 devices: a whole 8x8x8 slice. The times are simulated.
1024 devices in a mesh: gx: 8 (over y), gy: 4 (over x_hi), gz: 32 (over z, x_lo, core).
Axes of the slice: x: 8 (x_hi: 4, x_lo: 2; x = x_hi * 2 + x_lo), y: 8, z: 8, core: 2. Of those that a mesh axis runs over, the one named last changes fastest.
Arguments:
- trial: bfloat16 [16, 8, 128, 64, 128], P('gx', 'gy', 'gz'), may hold values from -6 to 6
- onsite: bfloat16 [16, 8, 128, 128, 128], P('gx', 'gy', 'gz'), as said below
- coupling: bfloat16 [3, 16, 8, 128, 128, 128], P(None, 'gx', 'gy', 'gz'), may hold values from -0.1875 to 0.1875
- bonds: int32 [3, 16, 8, 128], P(None, 'gx', 'gy', 'gz'), may hold values 0 or 1
Outputs:
- filtered: float32 [16, 8, 128, 64, 128], P('gx', 'gy', 'gz')
Inputs may be any that keep to these rules, and one draw needn't show every extreme that they name: `onsite`: each on-site block is symmetric in its last two dimensions.
All inputs are finite; a program needn't handle non-finite values. No bound on the sum of `bonds` on one device may be relied on, other than what follows from the above.
Results may differ from a plain program's by a relative error of at most 0.0052.
Values may be sent and summed in bfloat16 or wider, within the bound.
No kernel may reach another device: no remote copies, remote signals or barrier semaphores. Data moves between devices by JAX's collectives and lax.ppermute only.
A program may use at most 32 MiB of HBM per device.

v0:
```python
import jax
import jax.numpy as jnp
from jax import lax
from jax.sharding import PartitionSpec as P

STEPS = 5


center_shift = 0.25
half_inverse = 0.5


def passed_along(block, axis, distance):
    devices = range(lax.axis_size(axis))
    route = [(i - distance, i) for i in devices if i - distance in devices]
    return lax.ppermute(block, axis, route)


def block_apply(blocks, vecs):
    return jnp.einsum("...pq,...kq->...kp", blocks, vecs, preferred_element_type=jnp.float32)


def block_transposed(blocks, vecs):
    return jnp.einsum("...pq,...kp->...kq", blocks, vecs, preferred_element_type=jnp.float32)


def layer_of(array, axis, start, count):
    return lax.slice_in_dim(array, start, start + count, axis=axis)


def add_layers(total, axis, start, count, term):
    index = [slice(None)] * total.ndim
    index[axis] = slice(start, start + count)
    return total.at[tuple(index)].add(term)


def interior_terms(onsite, blocks, vecs):
    total = block_apply(onsite, vecs)
    for axis in range(3):
        length = vecs.shape[axis]
        own_blocks = layer_of(blocks[axis], axis, 0, length - 1)
        forward = block_apply(own_blocks, layer_of(vecs, axis, 1, length - 1))
        total = add_layers(total, axis, 0, length - 1, forward)
        backward = block_transposed(own_blocks, layer_of(vecs, axis, 0, length - 1))
        total = add_layers(total, axis, 1, length - 1, backward)
    return total


def returned_terms(onsite, blocks, vecs):
    lengths = (vecs.shape[0], vecs.shape[1], vecs.shape[2])
    tops = []
    upwards = []
    for axis in range(3):
        top_blocks = layer_of(blocks[axis], axis, lengths[axis] - 1, 1)
        tops.append(top_blocks)
        upwards.append(block_transposed(top_blocks, layer_of(vecs, axis, lengths[axis] - 1, 1)))
    above_x = passed_along(layer_of(vecs, 0, 0, 1), "gx", -1)
    above_y = passed_along(layer_of(vecs, 1, 0, 1), "gy", -1)
    above_z = passed_along(layer_of(vecs, 2, 0, 1), "gz", -1)
    below_x = passed_along(upwards[0], "gx", 1)
    below_y = passed_along(upwards[1], "gy", 1)
    below_z = passed_along(upwards[2], "gz", 1)
    above = (above_x, above_y, above_z)
    below = (below_x, below_y, below_z)
    total = interior_terms(onsite, blocks, vecs)
    for axis in range(3):
        total = add_layers(total, axis, lengths[axis] - 1, 1, block_apply(tops[axis], above[axis]))
        total = add_layers(total, axis, 0, 1, below[axis])
    return total


def shards(trial, onsite, coupling, bonds):
    blocks = coupling * bonds.astype(jnp.bfloat16)[..., None, None]

    def apply_operator(vecs):
        return returned_terms(onsite, blocks, vecs)

    def scaled(vecs):
        return half_inverse * (apply_operator(vecs) - center_shift * vecs.astype(jnp.float32))

    previous = trial
    current = scaled(trial).astype(jnp.bfloat16)
    for step in range(STEPS - 2):
        following = (2.0 * scaled(current) - previous.astype(jnp.float32)).astype(jnp.bfloat16)
        previous = current
        current = following
    return 2.0 * scaled(current) - previous.astype(jnp.float32)


def solution(mesh):
    placed = (
        P("gx", "gy", "gz", None, None),
        P("gx", "gy", "gz", None, None),
        P(None, "gx", "gy", "gz", None, None),
        P(None, "gx", "gy", "gz"),
    )
    return jax.shard_map(
        shards,
        mesh=mesh,
        in_specs=placed,
        out_specs=P("gx", "gy", "gz", None, None),
        check_vma=False,
    )
```

profile of v0, /device:TPU:439, one launch (start us, length us, event | category | flops | bytes accessed | tf_op | source)
XLA Modules:
  0.0 157.6 jit_solution(18364767654951135853)
XLA Ops:
  0.0 1.0 slice.2264
  1.0 2.0 %collective-permute-start = (bf16[1,2,4,64,128]{4,3,2,1,0:T(8,128)(2,1)S(1)}, bf16[1,2,4,64,128]{4,3,2,1,0:T(8,128)(2,1)S(1)}, u32[]{:S(2)}, u32[]{:S(2)}) collective-permute-start(bf16[1,2,4,64,128]{4,3,2,1,0:T(8,128)(2,1)S(1)} %slice.2264), channel_id=1, source_target_pairs={{128,0},{256,128},{384,256},{512,384},{640,512},{768,640},{896,768... | collective-permute-start | bytes 393224 | tf_op jit(solution)/shard_map/ppermute | solution.py:16
  2.9 0.7 convert_element_type.34
  3.7 1.6 %broadcast_multiply_fusion = bf16[3,2,2,4,128,128]{5,4,3,2,1,0:T(8,128)(2,1)S(1)} fusion(bf16[3,2,2,4,128,128]{5,4,3,2,1,0:T(8,128)(2,1)} %param.126, bf16[3,2,2,4]{3,2,1,0:T(2,128)(2,1)S(1)} %convert_element_type.34), kind=kLoop, calls=%fused_computation.122 | loop fusion | flops 786432 | bytes 3145824 | tf_op jit(solution)/shard_map/mul | solution.py:73
  5.5 4.5 %collective-permute-start.1 = (f32[1,2,4,64,128]{4,3,2,1,0:T(8,128)S(1)}, f32[1,2,4,64,128]{4,3,2,1,0:T(8,128)S(1)}, u32[]{:S(2)}, u32[]{:S(2)}) collective-permute-start(f32[1,2,4,64,128]{4,3,2,1,0:T(8,128)S(1)} %convolution_bitcast_fusion.3), channel_id=1, source_target_pairs={{0,128},{128,256},{256,384},{384,512},{512,640},{640,768},{768,896... | collective-permute-start | bytes 786440 | tf_op jit(solution)/shard_map/ppermute | solution.py:16
  10.0 2.1 %collective-permute-start.2 = (bf16[2,1,4,64,128]{4,3,2,0,1:T(8,128)(2,1)S(1)}, bf16[2,1,4,64,128]{4,3,2,0,1:T(8,128)(2,1)S(1)}, u32[]{:S(2)}, u32[]{:S(2)}) collective-permute-start(bf16[2,1,4,64,128]{4,3,2,0,1:T(8,128)(2,1)S(1)} %slice_bitcast_fusion.31), channel_id=1, source_target_pairs={{32,0},{64,32},{96,64},{33,1},{65,33},{97,65},{34,2},{66,34},{98,6... | collective-permute-start | bytes 393224 | tf_op jit(solution)/shard_map/ppermute | solution.py:16
  12.5 5.3 %collective-permute-start.3 = (f32[2,1,4,64,128]{4,3,2,1,0:T(8,128)S(1)}, f32[2,1,4,64,128]{4,3,2,1,0:T(8,128)S(1)}, u32[]{:S(2)}, u32[]{:S(2)}) collective-permute-start(f32[2,1,4,64,128]{4,3,2,1,0:T(8,128)S(1)} %convolution_bitcast_fusion.2), channel_id=1, source_target_pairs={{0,32},{32,64},{64,96},{1,33},{33,65},{65,97},{2,34},{34,66},{66,9... | collective-permute-start | bytes 786440 | tf_op jit(solution)/shard_map/ppermute | solution.py:16
  17.7 3.7 %collective-permute-start.4 = (bf16[2,2,1,64,128]{4,3,1,0,2:T(8,128)(2,1)S(1)}, bf16[2,2,1,64,128]{4,3,1,0,2:T(8,128)(2,1)S(1)}, u32[]{:S(2)}, u32[]{:S(2)}) collective-permute-start(bf16[2,2,1,64,128]{4,3,1,0,2:T(8,128)(2,1)S(1)} %slice_bitcast_fusion.40), channel_id=1, source_target_pairs={{1,0},{2,1},{3,2},{4,3},{5,4},{6,5},{7,6},{8,7},{9,8},{10,9},{11,1... | collective-permute-start | bytes 196616 | tf_op jit(solution)/shard_map/ppermute | solution.py:16
  21.5 0.5 fusion.172
  21.9 0.3 fusion.57
  22.4 0.3 fusion.59
  23.0 0.4 fusion.3
  23.8 6.0 %collective-permute-start.5 = (f32[2,2,1,64,128]{4,3,2,1,0:T(8,128)S(1)}, f32[2,2,1,64,128]{4,3,2,1,0:T(8,128)S(1)}, u32[]{:S(2)}, u32[]{:S(2)}) collective-permute-start(f32[2,2,1,64,128]{4,3,2,1,0:T(8,128)S(1)} %convolution_bitcast_fusion.42), channel_id=1, source_target_pairs={{0,1},{1,2},{2,3},{3,4},{4,5},{5,6},{6,7},{7,8},{8,9},{9,10},{10,1... | collective-permute-start | bytes 393224 | tf_op jit(solution)/shard_map/ppermute | solution.py:16
  30.5 5.6 %collective-permute-done.4 = bf16[2,2,1,64,128]{4,3,1,0,2:T(8,128)(2,1)S(1)} collective-permute-done((bf16[2,2,1,64,128]{4,3,1,0,2:T(8,128)(2,1)S(1)}, bf16[2,2,1,64,128]{4,3,1,0,2:T(8,128)(2,1)S(1)}, u32[]{:S(2)}, u32[]{:S(2)}) %collective-permute-start.4) | collective-permute-done | bytes 65568 | tf_op jit(solution)/shard_map/ppermute | solution.py:16
  36.5 0.5 fusion.173
  37.2 0.3 fusion.55
  37.7 0.3 fusion.51
  38.2 0.4 fusion.11
  38.9 1.9 %collective-permute-start.6 = (bf16[1,2,4,64,128]{4,3,2,1,0:T(8,128)(2,1)S(1)}, bf16[1,2,4,64,128]{4,3,2,1,0:T(8,128)(2,1)S(1)}, u32[]{:S(2)}, u32[]{:S(2)}) collective-permute-start(bf16[1,2,4,64,128]{4,3,2,1,0:T(8,128)(2,1)S(1)} %slice.2391), channel_id=1, source_target_pairs={{128,0},{256,128},{384,256},{512,384},{640,512},{768,640},{896,768... | collective-permute-start | bytes 393224 | tf_op jit(solution)/shard_map/ppermute | solution.py:16
  41.0 4.6 %collective-permute-start.7 = (f32[1,2,4,64,128]{4,3,2,1,0:T(8,128)S(1)}, f32[1,2,4,64,128]{4,3,2,1,0:T(8,128)S(1)}, u32[]{:S(2)}, u32[]{:S(2)}) collective-permute-start(f32[1,2,4,64,128]{4,3,2,1,0:T(8,128)S(1)} %convolution_bitcast_fusion.32), channel_id=1, source_target_pairs={{0,128},{128,256},{256,384},{384,512},{512,640},{640,768},{768,896... | collective-permute-start | bytes 786440 | tf_op jit(solution)/shard_map/ppermute | solution.py:16
  45.8 1.9 %collective-permute-start.8 = (bf16[2,1,4,64,128]{4,3,2,1,0:T(8,128)(2,1)S(1)}, bf16[2,1,4,64,128]{4,3,2,1,0:T(8,128)(2,1)S(1)}, u32[]{:S(2)}, u32[]{:S(2)}) collective-permute-start(bf16[2,1,4,64,128]{4,3,2,1,0:T(8,128)(2,1)S(1)} %slice.2395), channel_id=1, source_target_pairs={{32,0},{64,32},{96,64},{33,1},{65,33},{97,65},{34,2},{66,34},{98,6... | collective-permute-start | bytes 393224 | tf_op jit(solution)/shard_map/ppermute | solution.py:16
  47.7 5.5 %collective-permute-start.9 = (f32[2,1,4,64,128]{4,3,2,1,0:T(8,128)S(1)}, f32[2,1,4,64,128]{4,3,2,1,0:T(8,128)S(1)}, u32[]{:S(2)}, u32[]{:S(2)}) collective-permute-start(f32[2,1,4,64,128]{4,3,2,1,0:T(8,128)S(1)} %convolution_bitcast_fusion.30), channel_id=1, source_target_pairs={{0,32},{32,64},{64,96},{1,33},{33,65},{65,97},{2,34},{34,66},{66,9... | collective-permute-start | bytes 786440 | tf_op jit(solution)/shard_map/ppermute | solution.py:16
  53.2 1.9 %collective-permute-start.10 = (bf16[2,2,1,64,128]{4,3,2,1,0:T(8,128)(2,1)S(1)}, bf16[2,2,1,64,128]{4,3,2,1,0:T(8,128)(2,1)S(1)}, u32[]{:S(2)}, u32[]{:S(2)}) collective-permute-start(bf16[2,2,1,64,128]{4,3,2,1,0:T(8,128)(2,1)S(1)} %slice.2403), channel_id=1, source_target_pairs={{1,0},{2,1},{3,2},{4,3},{5,4},{6,5},{7,6},{8,7},{9,8},{10,9},{11,1... | collective-permute-start | bytes 196616 | tf_op jit(solution)/shard_map/ppermute | solution.py:16
  55.1 5.8 %collective-permute-start.11 = (f32[2,2,1,64,128]{4,3,2,1,0:T(8,128)S(1)}, f32[2,2,1,64,128]{4,3,2,1,0:T(8,128)S(1)}, u32[]{:S(2)}, u32[]{:S(2)}) collective-permute-start(f32[2,2,1,64,128]{4,3,2,1,0:T(8,128)S(1)} %convolution_bitcast_fusion.49), channel_id=1, source_target_pairs={{0,1},{1,2},{2,3},{3,4},{4,5},{5,6},{6,7},{7,8},{8,9},{9,10},{10,1... | collective-permute-start | bytes 393224 | tf_op jit(solution)/shard_map/ppermute | solution.py:16
  60.9 0.3 fusion.47
  61.3 0.3 fusion.81
  61.6 4.7 %collective-permute-done.10 = bf16[2,2,1,64,128]{4,3,2,1,0:T(8,128)(2,1)S(1)} collective-permute-done((bf16[2,2,1,64,128]{4,3,2,1,0:T(8,128)(2,1)S(1)}, bf16[2,2,1,64,128]{4,3,2,1,0:T(8,128)(2,1)S(1)}, u32[]{:S(2)}, u32[]{:S(2)}) %collective-permute-start.10) | collective-permute-done | bytes 65568 | tf_op jit(solution)/shard_map/ppermute | solution.py:16
  66.7 0.5 fusion.174
  67.4 0.3 fusion.45
  67.9 0.3 fusion.41
  68.5 0.4 fusion.9
  69.1 1.9 %collective-permute-start.12 = (bf16[1,2,4,64,128]{4,3,2,1,0:T(8,128)(2,1)S(1)}, bf16[1,2,4,64,128]{4,3,2,1,0:T(8,128)(2,1)S(1)}, u32[]{:S(2)}, u32[]{:S(2)}) collective-permute-start(bf16[1,2,4,64,128]{4,3,2,1,0:T(8,128)(2,1)S(1)} %slice.2409), channel_id=1, source_target_pairs={{128,0},{256,128},{384,256},{512,384},{640,512},{768,640},{896,768... | collective-permute-start | bytes 393224 | tf_op jit(solution)/shard_map/ppermute | solution.py:16
  71.2 4.6 %collective-permute-start.13 = (f32[1,2,4,64,128]{4,3,2,1,0:T(8,128)S(1)}, f32[1,2,4,64,128]{4,3,2,1,0:T(8,128)S(1)}, u32[]{:S(2)}, u32[]{:S(2)}) collective-permute-start(f32[1,2,4,64,128]{4,3,2,1,0:T(8,128)S(1)} %convolution_bitcast_fusion.24), channel_id=1, source_target_pairs={{0,128},{128,256},{256,384},{384,512},{512,640},{640,768},{768,896... | collective-permute-start | bytes 786440 | tf_op jit(solution)/shard_map/ppermute | solution.py:16
  76.0 1.9 %collective-permute-start.14 = (bf16[2,1,4,64,128]{4,3,2,1,0:T(8,128)(2,1)S(1)}, bf16[2,1,4,64,128]{4,3,2,1,0:T(8,128)(2,1)S(1)}, u32[]{:S(2)}, u32[]{:S(2)}) collective-permute-start(bf16[2,1,4,64,128]{4,3,2,1,0:T(8,128)(2,1)S(1)} %slice.2413), channel_id=1, source_target_pairs={{32,0},{64,32},{96,64},{33,1},{65,33},{97,65},{34,2},{66,34},{98,6... | collective-permute-start | bytes 393224 | tf_op jit(solution)/shard_map/ppermute | solution.py:16
  77.9 5.5 %collective-permute-start.15 = (f32[2,1,4,64,128]{4,3,2,1,0:T(8,128)S(1)}, f32[2,1,4,64,128]{4,3,2,1,0:T(8,128)S(1)}, u32[]{:S(2)}, u32[]{:S(2)}) collective-permute-start(f32[2,1,4,64,128]{4,3,2,1,0:T(8,128)S(1)} %convolution_bitcast_fusion.22), channel_id=1, source_target_pairs={{0,32},{32,64},{64,96},{1,33},{33,65},{65,97},{2,34},{34,66},{66,9... | collective-permute-start | bytes 786440 | tf_op jit(solution)/shard_map/ppermute | solution.py:16
  83.4 1.9 %collective-permute-start.16 = (bf16[2,2,1,64,128]{4,3,2,1,0:T(8,128)(2,1)S(1)}, bf16[2,2,1,64,128]{4,3,2,1,0:T(8,128)(2,1)S(1)}, u32[]{:S(2)}, u32[]{:S(2)}) collective-permute-start(bf16[2,2,1,64,128]{4,3,2,1,0:T(8,128)(2,1)S(1)} %slice.2421), channel_id=1, source_target_pairs={{1,0},{2,1},{3,2},{4,3},{5,4},{6,5},{7,6},{8,7},{9,8},{10,9},{11,1... | collective-permute-start | bytes 196616 | tf_op jit(solution)/shard_map/ppermute | solution.py:16
  85.4 5.8 %collective-permute-start.17 = (f32[2,2,1,64,128]{4,3,2,1,0:T(8,128)S(1)}, f32[2,2,1,64,128]{4,3,2,1,0:T(8,128)S(1)}, u32[]{:S(2)}, u32[]{:S(2)}) collective-permute-start(f32[2,2,1,64,128]{4,3,2,1,0:T(8,128)S(1)} %convolution_bitcast_fusion.47), channel_id=1, source_target_pairs={{0,1},{1,2},{2,3},{3,4},{4,5},{5,6},{6,7},{7,8},{8,9},{9,10},{10,1... | collective-permute-start | bytes 393224 | tf_op jit(solution)/shard_map/ppermute | solution.py:16
  91.1 0.3 fusion.37
  91.5 0.3 fusion.78
  91.9 4.7 %collective-permute-done.16 = bf16[2,2,1,64,128]{4,3,2,1,0:T(8,128)(2,1)S(1)} collective-permute-done((bf16[2,2,1,64,128]{4,3,2,1,0:T(8,128)(2,1)S(1)}, bf16[2,2,1,64,128]{4,3,2,1,0:T(8,128)(2,1)S(1)}, u32[]{:S(2)}, u32[]{:S(2)}) %collective-permute-start.16) | collective-permute-done | bytes 65568 | tf_op jit(solution)/shard_map/ppermute | solution.py:16
  97.0 0.5 fusion.175
  97.7 0.3 fusion.35
  98.7 0.4 fusion.7
  99.4 1.9 %collective-permute-start.18 = (bf16[1,2,4,64,128]{4,3,2,1,0:T(8,128)(2,1)S(1)}, bf16[1,2,4,64,128]{4,3,2,1,0:T(8,128)(2,1)S(1)}, u32[]{:S(2)}, u32[]{:S(2)}) collective-permute-start(bf16[1,2,4,64,128]{4,3,2,1,0:T(8,128)(2,1)S(1)} %slice.2427), channel_id=1, source_target_pairs={{128,0},{256,128},{384,256},{512,384},{640,512},{768,640},{896,768... | collective-permute-start | bytes 393224 | tf_op jit(solution)/shard_map/ppermute | solution.py:16
  101.5 4.6 %collective-permute-start.19 = (f32[1,2,4,64,128]{4,3,2,1,0:T(8,128)S(1)}, f32[1,2,4,64,128]{4,3,2,1,0:T(8,128)S(1)}, u32[]{:S(2)}, u32[]{:S(2)}) collective-permute-start(f32[1,2,4,64,128]{4,3,2,1,0:T(8,128)S(1)} %convolution_bitcast_fusion.16), channel_id=1, source_target_pairs={{0,128},{128,256},{256,384},{384,512},{512,640},{640,768},{768,896... | collective-permute-start | bytes 786440 | tf_op jit(solution)/shard_map/ppermute | solution.py:16
  106.3 1.9 %collective-permute-start.20 = (bf16[2,1,4,64,128]{4,3,2,1,0:T(8,128)(2,1)S(1)}, bf16[2,1,4,64,128]{4,3,2,1,0:T(8,128)(2,1)S(1)}, u32[]{:S(2)}, u32[]{:S(2)}) collective-permute-start(bf16[2,1,4,64,128]{4,3,2,1,0:T(8,128)(2,1)S(1)} %slice.2431), channel_id=1, source_target_pairs={{32,0},{64,32},{96,64},{33,1},{65,33},{97,65},{34,2},{66,34},{98,6... | collective-permute-start | bytes 393224 | tf_op jit(solution)/shard_map/ppermute | solution.py:16
  108.2 5.5 %collective-permute-start.21 = (f32[2,1,4,64,128]{4,3,2,1,0:T(8,128)S(1)}, f32[2,1,4,64,128]{4,3,2,1,0:T(8,128)S(1)}, u32[]{:S(2)}, u32[]{:S(2)}) collective-permute-start(f32[2,1,4,64,128]{4,3,2,1,0:T(8,128)S(1)} %convolution_bitcast_fusion.14), channel_id=1, source_target_pairs={{0,32},{32,64},{64,96},{1,33},{33,65},{65,97},{2,34},{34,66},{66,9... | collective-permute-start | bytes 786440 | tf_op jit(solution)/shard_map/ppermute | solution.py:16
  113.7 1.9 %collective-permute-start.22 = (bf16[2,2,1,64,128]{4,3,2,1,0:T(8,128)(2,1)S(1)}, bf16[2,2,1,64,128]{4,3,2,1,0:T(8,128)(2,1)S(1)}, u32[]{:S(2)}, u32[]{:S(2)}) collective-permute-start(bf16[2,2,1,64,128]{4,3,2,1,0:T(8,128)(2,1)S(1)} %slice.2439), channel_id=1, source_target_pairs={{1,0},{2,1},{3,2},{4,3},{5,4},{6,5},{7,6},{8,7},{9,8},{10,9},{11,1... | collective-permute-start | bytes 196616 | tf_op jit(solution)/shard_map/ppermute | solution.py:16
  115.6 5.8 %collective-permute-start.23 = (f32[2,2,1,64,128]{4,3,2,1,0:T(8,128)S(1)}, f32[2,2,1,64,128]{4,3,2,1,0:T(8,128)S(1)}, u32[]{:S(2)}, u32[]{:S(2)}) collective-permute-start(f32[2,2,1,64,128]{4,3,2,1,0:T(8,128)S(1)} %convolution_bitcast_fusion.45), channel_id=1, source_target_pairs={{0,1},{1,2},{2,3},{3,4},{4,5},{5,6},{6,7},{7,8},{8,9},{9,10},{10,1... | collective-permute-start | bytes 393224 | tf_op jit(solution)/shard_map/ppermute | solution.py:16
  121.4 0.3 fusion.27
  121.8 0.3 fusion.75
  122.1 4.4 %collective-permute-done.22 = bf16[2,2,1,64,128]{4,3,2,1,0:T(8,128)(2,1)S(1)} collective-permute-done((bf16[2,2,1,64,128]{4,3,2,1,0:T(8,128)(2,1)S(1)}, bf16[2,2,1,64,128]{4,3,2,1,0:T(8,128)(2,1)S(1)}, u32[]{:S(2)}, u32[]{:S(2)}) %collective-permute-start.22) | collective-permute-done | bytes 65568 | tf_op jit(solution)/shard_map/ppermute | solution.py:16
  126.9 0.5 fusion.176
  127.6 0.3 fusion.25
  128.6 0.4 fusion.5
  129.2 1.9 %collective-permute-start.24 = (bf16[1,2,4,64,128]{4,3,2,1,0:T(8,128)(2,1)S(1)}, bf16[1,2,4,64,128]{4,3,2,1,0:T(8,128)(2,1)S(1)}, u32[]{:S(2)}, u32[]{:S(2)}) collective-permute-start(bf16[1,2,4,64,128]{4,3,2,1,0:T(8,128)(2,1)S(1)} %slice.2445), channel_id=1, source_target_pairs={{128,0},{256,128},{384,256},{512,384},{640,512},{768,640},{896,768... | collective-permute-start | bytes 393224 | tf_op jit(solution)/shard_map/ppermute | solution.py:16
  131.4 4.6 %collective-permute-start.25 = (f32[1,2,4,64,128]{4,3,2,1,0:T(8,128)S(1)}, f32[1,2,4,64,128]{4,3,2,1,0:T(8,128)S(1)}, u32[]{:S(2)}, u32[]{:S(2)}) collective-permute-start(f32[1,2,4,64,128]{4,3,2,1,0:T(8,128)S(1)} %convolution_bitcast_fusion.8), channel_id=1, source_target_pairs={{0,128},{128,256},{256,384},{384,512},{512,640},{640,768},{768,896... | collective-permute-start | bytes 786440 | tf_op jit(solution)/shard_map/ppermute | solution.py:16
  136.1 1.9 %collective-permute-start.26 = (bf16[2,1,4,64,128]{4,3,2,1,0:T(8,128)(2,1)S(1)}, bf16[2,1,4,64,128]{4,3,2,1,0:T(8,128)(2,1)S(1)}, u32[]{:S(2)}, u32[]{:S(2)}) collective-permute-start(bf16[2,1,4,64,128]{4,3,2,1,0:T(8,128)(2,1)S(1)} %slice.2449), channel_id=1, source_target_pairs={{32,0},{64,32},{96,64},{33,1},{65,33},{97,65},{34,2},{66,34},{98,6... | collective-permute-start | bytes 393224 | tf_op jit(solution)/shard_map/ppermute | solution.py:16
  138.1 5.5 %collective-permute-start.27 = (f32[2,1,4,64,128]{4,3,2,1,0:T(8,128)S(1)}, f32[2,1,4,64,128]{4,3,2,1,0:T(8,128)S(1)}, u32[]{:S(2)}, u32[]{:S(2)}) collective-permute-start(f32[2,1,4,64,128]{4,3,2,1,0:T(8,128)S(1)} %convolution_bitcast_fusion.6), channel_id=1, source_target_pairs={{0,32},{32,64},{64,96},{1,33},{33,65},{65,97},{2,34},{34,66},{66,9... | collective-permute-start | bytes 786440 | tf_op jit(solution)/shard_map/ppermute | solution.py:16
  143.6 1.9 %collective-permute-start.28 = (bf16[2,2,1,64,128]{4,3,2,1,0:T(8,128)(2,1)S(1)}, bf16[2,2,1,64,128]{4,3,2,1,0:T(8,128)(2,1)S(1)}, u32[]{:S(2)}, u32[]{:S(2)}) collective-permute-start(bf16[2,2,1,64,128]{4,3,2,1,0:T(8,128)(2,1)S(1)} %slice.2457), channel_id=1, source_target_pairs={{1,0},{2,1},{3,2},{4,3},{5,4},{6,5},{7,6},{8,7},{9,8},{10,9},{11,1... | collective-permute-start | bytes 196616 | tf_op jit(solution)/shard_map/ppermute | solution.py:16
  145.5 5.8 %collective-permute-start.29 = (f32[2,2,1,64,128]{4,3,2,1,0:T(8,128)S(1)}, f32[2,2,1,64,128]{4,3,2,1,0:T(8,128)S(1)}, u32[]{:S(2)}, u32[]{:S(2)}) collective-permute-start(f32[2,2,1,64,128]{4,3,2,1,0:T(8,128)S(1)} %convolution_bitcast_fusion.43), channel_id=1, source_target_pairs={{0,1},{1,2},{2,3},{3,4},{4,5},{5,6},{6,7},{7,8},{8,9},{9,10},{10,1... | collective-permute-start | bytes 393224 | tf_op jit(solution)/shard_map/ppermute | solution.py:16
  151.3 0.3 fusion.17
  152.0 4.5 %collective-permute-done.28 = bf16[2,2,1,64,128]{4,3,2,1,0:T(8,128)(2,1)S(1)} collective-permute-done((bf16[2,2,1,64,128]{4,3,2,1,0:T(8,128)(2,1)S(1)}, bf16[2,2,1,64,128]{4,3,2,1,0:T(8,128)(2,1)S(1)}, u32[]{:S(2)}, u32[]{:S(2)}) %collective-permute-start.28) | collective-permute-done | bytes 65568 | tf_op jit(solution)/shard_map/ppermute | solution.py:16
  156.7 0.9 convert_subtract_fusion
  (103 shorter events, 10.2 us)
Async XLA Ops:
  0.0 21.5 %copy-start = (bf16[2,2,4,128,128]{4,3,2,1,0:T(8,128)(2,1)S(1)}, bf16[2,2,4,128,128]{4,3,2,1,0:T(8,128)(2,1)}, u32[]{:S(2)}) copy-start(bf16[2,2,4,128,128]{4,3,2,1,0:T(8,128)(2,1)} %param.125) | copy-start | bytes 1572868
  1.0 22.8 %collective-permute-start = (bf16[1,2,4,64,128]{4,3,2,1,0:T(8,128)(2,1)S(1)}, bf16[1,2,4,64,128]{4,3,2,1,0:T(8,128)(2,1)S(1)}, u32[]{:S(2)}, u32[]{:S(2)}) collective-permute-start(bf16[1,2,4,64,128]{4,3,2,1,0:T(8,128)(2,1)S(1)} %slice.2264), channel_id=1, source_target_pairs={{128,0},{256,128},{384,256},{512,384},{640,512},{768,640},{896,768... | collective-permute-start | bytes 393224 | tf_op jit(solution)/shard_map/ppermute | solution.py:16
  3.6 1.6 %copy-start.1 = (bf16[2,2,4,64,128]{4,3,2,1,0:T(8,128)(2,1)S(1)}, bf16[2,2,4,64,128]{4,3,2,1,0:T(8,128)(2,1)}, u32[]{:S(2)}) copy-start(bf16[2,2,4,64,128]{4,3,2,1,0:T(8,128)(2,1)} %param.124) | copy-start | bytes 786436
  5.5 24.6 %collective-permute-start.1 = (f32[1,2,4,64,128]{4,3,2,1,0:T(8,128)S(1)}, f32[1,2,4,64,128]{4,3,2,1,0:T(8,128)S(1)}, u32[]{:S(2)}, u32[]{:S(2)}) collective-permute-start(f32[1,2,4,64,128]{4,3,2,1,0:T(8,128)S(1)} %convolution_bitcast_fusion.3), channel_id=1, source_target_pairs={{0,128},{128,256},{256,384},{384,512},{512,640},{640,768},{768,896... | collective-permute-start | bytes 786440 | tf_op jit(solution)/shard_map/ppermute | solution.py:16
  10.0 20.1 %collective-permute-start.2 = (bf16[2,1,4,64,128]{4,3,2,0,1:T(8,128)(2,1)S(1)}, bf16[2,1,4,64,128]{4,3,2,0,1:T(8,128)(2,1)S(1)}, u32[]{:S(2)}, u32[]{:S(2)}) collective-permute-start(bf16[2,1,4,64,128]{4,3,2,0,1:T(8,128)(2,1)S(1)} %slice_bitcast_fusion.31), channel_id=1, source_target_pairs={{32,0},{64,32},{96,64},{33,1},{65,33},{97,65},{34,2},{66,34},{98,6... | collective-permute-start | bytes 393224 | tf_op jit(solution)/shard_map/ppermute | solution.py:16
  12.5 18.0 %collective-permute-start.3 = (f32[2,1,4,64,128]{4,3,2,1,0:T(8,128)S(1)}, f32[2,1,4,64,128]{4,3,2,1,0:T(8,128)S(1)}, u32[]{:S(2)}, u32[]{:S(2)}) collective-permute-start(f32[2,1,4,64,128]{4,3,2,1,0:T(8,128)S(1)} %convolution_bitcast_fusion.2), channel_id=1, source_target_pairs={{0,32},{32,64},{64,96},{1,33},{33,65},{65,97},{2,34},{34,66},{66,9... | collective-permute-start | bytes 786440 | tf_op jit(solution)/shard_map/ppermute | solution.py:16
  17.7 18.4 %collective-permute-start.4 = (bf16[2,2,1,64,128]{4,3,1,0,2:T(8,128)(2,1)S(1)}, bf16[2,2,1,64,128]{4,3,1,0,2:T(8,128)(2,1)S(1)}, u32[]{:S(2)}, u32[]{:S(2)}) collective-permute-start(bf16[2,2,1,64,128]{4,3,1,0,2:T(8,128)(2,1)S(1)} %slice_bitcast_fusion.40), channel_id=1, source_target_pairs={{1,0},{2,1},{3,2},{4,3},{5,4},{6,5},{7,6},{8,7},{9,8},{10,9},{11,1... | collective-permute-start | bytes 196616 | tf_op jit(solution)/shard_map/ppermute | solution.py:16
  23.8 12.6 %collective-permute-start.5 = (f32[2,2,1,64,128]{4,3,2,1,0:T(8,128)S(1)}, f32[2,2,1,64,128]{4,3,2,1,0:T(8,128)S(1)}, u32[]{:S(2)}, u32[]{:S(2)}) collective-permute-start(f32[2,2,1,64,128]{4,3,2,1,0:T(8,128)S(1)} %convolution_bitcast_fusion.42), channel_id=1, source_target_pairs={{0,1},{1,2},{2,3},{3,4},{4,5},{5,6},{6,7},{7,8},{8,9},{9,10},{10,1... | collective-permute-start | bytes 393224 | tf_op jit(solution)/shard_map/ppermute | solution.py:16
  38.9 16.2 %collective-permute-start.6 = (bf16[1,2,4,64,128]{4,3,2,1,0:T(8,128)(2,1)S(1)}, bf16[1,2,4,64,128]{4,3,2,1,0:T(8,128)(2,1)S(1)}, u32[]{:S(2)}, u32[]{:S(2)}) collective-permute-start(bf16[1,2,4,64,128]{4,3,2,1,0:T(8,128)(2,1)S(1)} %slice.2391), channel_id=1, source_target_pairs={{128,0},{256,128},{384,256},{512,384},{640,512},{768,640},{896,768... | collective-permute-start | bytes 393224 | tf_op jit(solution)/shard_map/ppermute | solution.py:16
  41.0 20.2 %collective-permute-start.7 = (f32[1,2,4,64,128]{4,3,2,1,0:T(8,128)S(1)}, f32[1,2,4,64,128]{4,3,2,1,0:T(8,128)S(1)}, u32[]{:S(2)}, u32[]{:S(2)}) collective-permute-start(f32[1,2,4,64,128]{4,3,2,1,0:T(8,128)S(1)} %convolution_bitcast_fusion.32), channel_id=1, source_target_pairs={{0,128},{128,256},{256,384},{384,512},{512,640},{640,768},{768,896... | collective-permute-start | bytes 786440 | tf_op jit(solution)/shard_map/ppermute | solution.py:16
  45.8 15.5 %collective-permute-start.8 = (bf16[2,1,4,64,128]{4,3,2,1,0:T(8,128)(2,1)S(1)}, bf16[2,1,4,64,128]{4,3,2,1,0:T(8,128)(2,1)S(1)}, u32[]{:S(2)}, u32[]{:S(2)}) collective-permute-start(bf16[2,1,4,64,128]{4,3,2,1,0:T(8,128)(2,1)S(1)} %slice.2395), channel_id=1, source_target_pairs={{32,0},{64,32},{96,64},{33,1},{65,33},{97,65},{34,2},{66,34},{98,6... | collective-permute-start | bytes 393224 | tf_op jit(solution)/shard_map/ppermute | solution.py:16
  47.7 13.9 %collective-permute-start.9 = (f32[2,1,4,64,128]{4,3,2,1,0:T(8,128)S(1)}, f32[2,1,4,64,128]{4,3,2,1,0:T(8,128)S(1)}, u32[]{:S(2)}, u32[]{:S(2)}) collective-permute-start(f32[2,1,4,64,128]{4,3,2,1,0:T(8,128)S(1)} %convolution_bitcast_fusion.30), channel_id=1, source_target_pairs={{0,32},{32,64},{64,96},{1,33},{33,65},{65,97},{2,34},{34,66},{66,9... | collective-permute-start | bytes 786440 | tf_op jit(solution)/shard_map/ppermute | solution.py:16
  53.2 13.2 %collective-permute-start.10 = (bf16[2,2,1,64,128]{4,3,2,1,0:T(8,128)(2,1)S(1)}, bf16[2,2,1,64,128]{4,3,2,1,0:T(8,128)(2,1)S(1)}, u32[]{:S(2)}, u32[]{:S(2)}) collective-permute-start(bf16[2,2,1,64,128]{4,3,2,1,0:T(8,128)(2,1)S(1)} %slice.2403), channel_id=1, source_target_pairs={{1,0},{2,1},{3,2},{4,3},{5,4},{6,5},{7,6},{8,7},{9,8},{10,9},{11,1... | collective-permute-start | bytes 196616 | tf_op jit(solution)/shard_map/ppermute | solution.py:16
  55.1 11.5 %collective-permute-start.11 = (f32[2,2,1,64,128]{4,3,2,1,0:T(8,128)S(1)}, f32[2,2,1,64,128]{4,3,2,1,0:T(8,128)S(1)}, u32[]{:S(2)}, u32[]{:S(2)}) collective-permute-start(f32[2,2,1,64,128]{4,3,2,1,0:T(8,128)S(1)} %convolution_bitcast_fusion.49), channel_id=1, source_target_pairs={{0,1},{1,2},{2,3},{3,4},{4,5},{5,6},{6,7},{7,8},{8,9},{9,10},{10,1... | collective-permute-start | bytes 393224 | tf_op jit(solution)/shard_map/ppermute | solution.py:16
  69.1 16.2 %collective-permute-start.12 = (bf16[1,2,4,64,128]{4,3,2,1,0:T(8,128)(2,1)S(1)}, bf16[1,2,4,64,128]{4,3,2,1,0:T(8,128)(2,1)S(1)}, u32[]{:S(2)}, u32[]{:S(2)}) collective-permute-start(bf16[1,2,4,64,128]{4,3,2,1,0:T(8,128)(2,1)S(1)} %slice.2409), channel_id=1, source_target_pairs={{128,0},{256,128},{384,256},{512,384},{640,512},{768,640},{896,768... | collective-permute-start | bytes 393224 | tf_op jit(solution)/shard_map/ppermute | solution.py:16
  71.2 20.2 %collective-permute-start.13 = (f32[1,2,4,64,128]{4,3,2,1,0:T(8,128)S(1)}, f32[1,2,4,64,128]{4,3,2,1,0:T(8,128)S(1)}, u32[]{:S(2)}, u32[]{:S(2)}) collective-permute-start(f32[1,2,4,64,128]{4,3,2,1,0:T(8,128)S(1)} %convolution_bitcast_fusion.24), channel_id=1, source_target_pairs={{0,128},{128,256},{256,384},{384,512},{512,640},{640,768},{768,896... | collective-permute-start | bytes 786440 | tf_op jit(solution)/shard_map/ppermute | solution.py:16
  76.0 15.5 %collective-permute-start.14 = (bf16[2,1,4,64,128]{4,3,2,1,0:T(8,128)(2,1)S(1)}, bf16[2,1,4,64,128]{4,3,2,1,0:T(8,128)(2,1)S(1)}, u32[]{:S(2)}, u32[]{:S(2)}) collective-permute-start(bf16[2,1,4,64,128]{4,3,2,1,0:T(8,128)(2,1)S(1)} %slice.2413), channel_id=1, source_target_pairs={{32,0},{64,32},{96,64},{33,1},{65,33},{97,65},{34,2},{66,34},{98,6... | collective-permute-start | bytes 393224 | tf_op jit(solution)/shard_map/ppermute | solution.py:16
  77.9 13.9 %collective-permute-start.15 = (f32[2,1,4,64,128]{4,3,2,1,0:T(8,128)S(1)}, f32[2,1,4,64,128]{4,3,2,1,0:T(8,128)S(1)}, u32[]{:S(2)}, u32[]{:S(2)}) collective-permute-start(f32[2,1,4,64,128]{4,3,2,1,0:T(8,128)S(1)} %convolution_bitcast_fusion.22), channel_id=1, source_target_pairs={{0,32},{32,64},{64,96},{1,33},{33,65},{65,97},{2,34},{34,66},{66,9... | collective-permute-start | bytes 786440 | tf_op jit(solution)/shard_map/ppermute | solution.py:16
  83.4 13.2 %collective-permute-start.16 = (bf16[2,2,1,64,128]{4,3,2,1,0:T(8,128)(2,1)S(1)}, bf16[2,2,1,64,128]{4,3,2,1,0:T(8,128)(2,1)S(1)}, u32[]{:S(2)}, u32[]{:S(2)}) collective-permute-start(bf16[2,2,1,64,128]{4,3,2,1,0:T(8,128)(2,1)S(1)} %slice.2421), channel_id=1, source_target_pairs={{1,0},{2,1},{3,2},{4,3},{5,4},{6,5},{7,6},{8,7},{9,8},{10,9},{11,1... | collective-permute-start | bytes 196616 | tf_op jit(solution)/shard_map/ppermute | solution.py:16
  85.4 11.5 %collective-permute-start.17 = (f32[2,2,1,64,128]{4,3,2,1,0:T(8,128)S(1)}, f32[2,2,1,64,128]{4,3,2,1,0:T(8,128)S(1)}, u32[]{:S(2)}, u32[]{:S(2)}) collective-permute-start(f32[2,2,1,64,128]{4,3,2,1,0:T(8,128)S(1)} %convolution_bitcast_fusion.47), channel_id=1, source_target_pairs={{0,1},{1,2},{2,3},{3,4},{4,5},{5,6},{6,7},{7,8},{8,9},{9,10},{10,1... | collective-permute-start | bytes 393224 | tf_op jit(solution)/shard_map/ppermute | solution.py:16
  99.4 16.2 %collective-permute-start.18 = (bf16[1,2,4,64,128]{4,3,2,1,0:T(8,128)(2,1)S(1)}, bf16[1,2,4,64,128]{4,3,2,1,0:T(8,128)(2,1)S(1)}, u32[]{:S(2)}, u32[]{:S(2)}) collective-permute-start(bf16[1,2,4,64,128]{4,3,2,1,0:T(8,128)(2,1)S(1)} %slice.2427), channel_id=1, source_target_pairs={{128,0},{256,128},{384,256},{512,384},{640,512},{768,640},{896,768... | collective-permute-start | bytes 393224 | tf_op jit(solution)/shard_map/ppermute | solution.py:16
  101.5 20.2 %collective-permute-start.19 = (f32[1,2,4,64,128]{4,3,2,1,0:T(8,128)S(1)}, f32[1,2,4,64,128]{4,3,2,1,0:T(8,128)S(1)}, u32[]{:S(2)}, u32[]{:S(2)}) collective-permute-start(f32[1,2,4,64,128]{4,3,2,1,0:T(8,128)S(1)} %convolution_bitcast_fusion.16), channel_id=1, source_target_pairs={{0,128},{128,256},{256,384},{384,512},{512,640},{640,768},{768,896... | collective-permute-start | bytes 786440 | tf_op jit(solution)/shard_map/ppermute | solution.py:16
  106.3 15.5 %collective-permute-start.20 = (bf16[2,1,4,64,128]{4,3,2,1,0:T(8,128)(2,1)S(1)}, bf16[2,1,4,64,128]{4,3,2,1,0:T(8,128)(2,1)S(1)}, u32[]{:S(2)}, u32[]{:S(2)}) collective-permute-start(bf16[2,1,4,64,128]{4,3,2,1,0:T(8,128)(2,1)S(1)} %slice.2431), channel_id=1, source_target_pairs={{32,0},{64,32},{96,64},{33,1},{65,33},{97,65},{34,2},{66,34},{98,6... | collective-permute-start | bytes 393224 | tf_op jit(solution)/shard_map/ppermute | solution.py:16
  108.2 13.9 %collective-permute-start.21 = (f32[2,1,4,64,128]{4,3,2,1,0:T(8,128)S(1)}, f32[2,1,4,64,128]{4,3,2,1,0:T(8,128)S(1)}, u32[]{:S(2)}, u32[]{:S(2)}) collective-permute-start(f32[2,1,4,64,128]{4,3,2,1,0:T(8,128)S(1)} %convolution_bitcast_fusion.14), channel_id=1, source_target_pairs={{0,32},{32,64},{64,96},{1,33},{33,65},{65,97},{2,34},{34,66},{66,9... | collective-permute-start | bytes 786440 | tf_op jit(solution)/shard_map/ppermute | solution.py:16
  113.7 12.8 %collective-permute-start.22 = (bf16[2,2,1,64,128]{4,3,2,1,0:T(8,128)(2,1)S(1)}, bf16[2,2,1,64,128]{4,3,2,1,0:T(8,128)(2,1)S(1)}, u32[]{:S(2)}, u32[]{:S(2)}) collective-permute-start(bf16[2,2,1,64,128]{4,3,2,1,0:T(8,128)(2,1)S(1)} %slice.2439), channel_id=1, source_target_pairs={{1,0},{2,1},{3,2},{4,3},{5,4},{6,5},{7,6},{8,7},{9,8},{10,9},{11,1... | collective-permute-start | bytes 196616 | tf_op jit(solution)/shard_map/ppermute | solution.py:16
  115.6 11.1 %collective-permute-start.23 = (f32[2,2,1,64,128]{4,3,2,1,0:T(8,128)S(1)}, f32[2,2,1,64,128]{4,3,2,1,0:T(8,128)S(1)}, u32[]{:S(2)}, u32[]{:S(2)}) collective-permute-start(f32[2,2,1,64,128]{4,3,2,1,0:T(8,128)S(1)} %convolution_bitcast_fusion.45), channel_id=1, source_target_pairs={{0,1},{1,2},{2,3},{3,4},{4,5},{5,6},{6,7},{7,8},{8,9},{9,10},{10,1... | collective-permute-start | bytes 393224 | tf_op jit(solution)/shard_map/ppermute | solution.py:16
  129.2 16.2 %collective-permute-start.24 = (bf16[1,2,4,64,128]{4,3,2,1,0:T(8,128)(2,1)S(1)}, bf16[1,2,4,64,128]{4,3,2,1,0:T(8,128)(2,1)S(1)}, u32[]{:S(2)}, u32[]{:S(2)}) collective-permute-start(bf16[1,2,4,64,128]{4,3,2,1,0:T(8,128)(2,1)S(1)} %slice.2445), channel_id=1, source_target_pairs={{128,0},{256,128},{384,256},{512,384},{640,512},{768,640},{896,768... | collective-permute-start | bytes 393224 | tf_op jit(solution)/shard_map/ppermute | solution.py:16
  131.4 20.2 %collective-permute-start.25 = (f32[1,2,4,64,128]{4,3,2,1,0:T(8,128)S(1)}, f32[1,2,4,64,128]{4,3,2,1,0:T(8,128)S(1)}, u32[]{:S(2)}, u32[]{:S(2)}) collective-permute-start(f32[1,2,4,64,128]{4,3,2,1,0:T(8,128)S(1)} %convolution_bitcast_fusion.8), channel_id=1, source_target_pairs={{0,128},{128,256},{256,384},{384,512},{512,640},{640,768},{768,896... | collective-permute-start | bytes 786440 | tf_op jit(solution)/shard_map/ppermute | solution.py:16
  136.1 15.5 %collective-permute-start.26 = (bf16[2,1,4,64,128]{4,3,2,1,0:T(8,128)(2,1)S(1)}, bf16[2,1,4,64,128]{4,3,2,1,0:T(8,128)(2,1)S(1)}, u32[]{:S(2)}, u32[]{:S(2)}) collective-permute-start(bf16[2,1,4,64,128]{4,3,2,1,0:T(8,128)(2,1)S(1)} %slice.2449), channel_id=1, source_target_pairs={{32,0},{64,32},{96,64},{33,1},{65,33},{97,65},{34,2},{66,34},{98,6... | collective-permute-start | bytes 393224 | tf_op jit(solution)/shard_map/ppermute | solution.py:16
  138.1 13.9 %collective-permute-start.27 = (f32[2,1,4,64,128]{4,3,2,1,0:T(8,128)S(1)}, f32[2,1,4,64,128]{4,3,2,1,0:T(8,128)S(1)}, u32[]{:S(2)}, u32[]{:S(2)}) collective-permute-start(f32[2,1,4,64,128]{4,3,2,1,0:T(8,128)S(1)} %convolution_bitcast_fusion.6), channel_id=1, source_target_pairs={{0,32},{32,64},{64,96},{1,33},{33,65},{65,97},{2,34},{34,66},{66,9... | collective-permute-start | bytes 786440 | tf_op jit(solution)/shard_map/ppermute | solution.py:16
  143.6 12.9 %collective-permute-start.28 = (bf16[2,2,1,64,128]{4,3,2,1,0:T(8,128)(2,1)S(1)}, bf16[2,2,1,64,128]{4,3,2,1,0:T(8,128)(2,1)S(1)}, u32[]{:S(2)}, u32[]{:S(2)}) collective-permute-start(bf16[2,2,1,64,128]{4,3,2,1,0:T(8,128)(2,1)S(1)} %slice.2457), channel_id=1, source_target_pairs={{1,0},{2,1},{3,2},{4,3},{5,4},{6,5},{7,6},{8,7},{9,8},{10,9},{11,1... | collective-permute-start | bytes 196616 | tf_op jit(solution)/shard_map/ppermute | solution.py:16
  145.5 11.2 %collective-permute-start.29 = (f32[2,2,1,64,128]{4,3,2,1,0:T(8,128)S(1)}, f32[2,2,1,64,128]{4,3,2,1,0:T(8,128)S(1)}, u32[]{:S(2)}, u32[]{:S(2)}) collective-permute-start(f32[2,2,1,64,128]{4,3,2,1,0:T(8,128)S(1)} %convolution_bitcast_fusion.43), channel_id=1, source_target_pairs={{0,1},{1,2},{2,3},{3,4},{4,5},{5,6},{6,7},{7,8},{8,9},{9,10},{10,1... | collective-permute-start | bytes 393224 | tf_op jit(solution)/shard_map/ppermute | solution.py:16
where the time goes:
time: 159 us; the launch traced here: 158 us
  starting transfers between devices  110 us (69%)
  waiting for transfers between devices  24 us (15%)
  matrix products  17.1 us (11%)
  other arithmetic  4.45 us (3%)
    ppermute x30, starting transfers between devices, passed_along(): return lax.ppermute(block, axis, route)  110 us
    ppermute x30, waiting for transfers between devices, passed_along(): return lax.ppermute(block, axis, route)  24 us
    dot_general x35, matrix products, block_apply(): jnp.einsum('...pq,...kq->...kp', blocks, vecs, preferred_element_type=jnp...  10.9 us
    dot_general x30, matrix products, block_transposed(): jnp.einsum('...pq,...kp->...kq', blocks, vecs, preferred_element_type=jnp...  6.15 us
  transfers between devices with their start and end apart: 30, of which 5 were waited for; matrix products, arithmetic and copies ran while one was open for 7% of the time, Pallas kernels for 0%

commit v1 on v0

v1 whole, which is shorter than its diff:
```python
import jax
import jax.numpy as jnp
from jax import lax
from jax.experimental import pallas as pl
from jax.experimental.pallas import tpu as pltpu
from jax.sharding import PartitionSpec as P


STEPS = 5
CENTER_SHIFT = 0.25
HALF_INVERSE = 0.5

F32 = jnp.float32
BF16 = jnp.bfloat16
AXES = ("gx", "gy", "gz")


def places(lengths):
    nx, ny, nz = lengths
    return [(x, y, z) for x in range(nx) for y in range(ny) for z in range(nz)]


def number(place, lengths):
    return (place[0] * lengths[1] + place[1]) * lengths[2] + place[2]


def stepped(place, axis, by):
    moved = list(place)
    moved[axis] += by
    return tuple(moved)


def face(lengths, axis, layer):
    return [number(p, lengths) for p in places(lengths) if p[axis] == layer]


def plain(vecs, blocks):
    left = vecs[0] if len(vecs) == 1 else jnp.concatenate(vecs, axis=1)
    right = blocks[0] if len(blocks) == 1 else jnp.concatenate(blocks, axis=0)
    return lax.dot_general(left, right, (((1,), (0,)), ((), ())), preferred_element_type=F32)


def crossed(vecs, blocks):
    left = vecs[0] if len(vecs) == 1 else jnp.concatenate(vecs, axis=1)
    right = blocks[0] if len(blocks) == 1 else jnp.concatenate(blocks, axis=1)
    return lax.dot_general(left, right, (((1,), (1,)), ((), ())), preferred_element_type=F32)


def is_even_on(axis):
    return lax.rem(lax.axis_index(AXES[axis]), 2) == 0


def write_messages(lengths, vecs, blocks, sends):
    for axis in range(3):
        low = face(lengths, axis, 0)
        top = face(lengths, axis, lengths[axis] - 1)
        first, second = sends[2 * axis], sends[2 * axis + 1]
        is_even = is_even_on(axis)
        for i in range(len(top)):
            term = plain([vecs[top[i]]], [blocks[axis, top[i]]])
            below = vecs[low[i]].astype(F32)
            first[i] = jnp.where(is_even, term, below).astype(BF16)
            second[i] = jnp.where(is_even, below, term).astype(BF16)


def prepare(lengths, bonds, trial, coupling, blocks, *sends):
    for axis in range(3):
        for p in places(lengths):
            c = number(p, lengths)
            blocks[axis, c] = coupling[axis, c] * bonds[axis, p[0], p[1], p[2]].astype(F32).astype(BF16)
    write_messages(lengths, trial, blocks, sends)


def interior(lengths, vecs, onsite, blocks, total):
    for p in places(lengths):
        c = number(p, lengths)
        vs, ms, ws, ns = [vecs[c]], [onsite[c]], [], []
        for axis in range(3):
            if p[axis] > 0:
                lower = number(stepped(p, axis, -1), lengths)
                vs.append(vecs[lower])
                ms.append(blocks[axis, lower])
            if p[axis] < lengths[axis] - 1:
                upper = number(stepped(p, axis, 1), lengths)
                ws.append(vecs[upper])
                ns.append(blocks[axis, c])
        inside = plain(vs, ms)
        total[c] = inside + crossed(ws, ns) if ws else inside


def finish(lengths, step, total, vecs, previous, blocks, *refs):
    got, result, sends = refs[:6], refs[6], refs[7:]
    evens = [is_even_on(axis) for axis in range(3)]
    for p in places(lengths):
        c = number(p, lengths)
        value = total[c]
        ws, ns = [], []
        for axis in range(3):
            is_even = evens[axis]
            first, second = got[2 * axis], got[2 * axis + 1]
            if p[axis] == lengths[axis] - 1:
                i = face(lengths, axis, p[axis]).index(c)
                ws.append(jnp.where(is_even, first[i], second[i]))
                ns.append(blocks[axis, c])
            if p[axis] == 0:
                i = face(lengths, axis, 0).index(c)
                value = value + jnp.where(is_even, second[i], first[i]).astype(F32)
        if ws:
            value = value + crossed(ws, ns)
        shifted = value - CENTER_SHIFT * vecs[c].astype(F32)
        if step == 0:
            following = HALF_INVERSE * shifted
        else:
            following = 2.0 * HALF_INVERSE * shifted - previous[c].astype(F32)
        result[c] = following.astype(result.dtype)
    if sends:
        write_messages(lengths, result, blocks, sends)


def call(body, operands, scalars, shapes, flops):
    in_specs = [pl.BlockSpec(memory_space=pltpu.SMEM)] * len(scalars)
    in_specs += [pl.BlockSpec(memory_space=pltpu.VMEM)] * len(operands)
    moved = sum(a.size * a.dtype.itemsize for a in operands) + sum(s.size * s.dtype.itemsize for s in shapes)
    return pl.pallas_call(
        body,
        out_shape=shapes,
        in_specs=in_specs,
        out_specs=[pl.BlockSpec(memory_space=pltpu.VMEM)] * len(shapes),
        cost_estimate=pl.CostEstimate(flops=flops, bytes_accessed=moved, transcendentals=0),
        compiler_params=pltpu.CompilerParams(vmem_limit_bytes=24 << 20),
    )(*scalars, *operands)


def routes(axis):
    n = lax.axis_size(axis)
    pairs = [(i, i + 1) for i in range(0, n - 1, 2)]
    others = [(i, i + 1) for i in range(1, n - 1, 2)]
    both = lambda links: links + [(j, i) for i, j in links]
    return both(pairs), both(others)


def exchanged(sends):
    got = []
    for axis in range(3):
        for which, route in enumerate(routes(AXES[axis])):
            got.append(lax.ppermute(sends[2 * axis + which], AXES[axis], route))
    return got


def shards(trial, onsite, coupling, bonds):
    lengths = trial.shape[:3]
    k, q = trial.shape[3:]
    cells = lengths[0] * lengths[1] * lengths[2]
    vecs = trial.reshape(cells, k, q)
    onsite = onsite.reshape(cells, q, q)
    coupling = coupling.reshape(3, cells, q, q)
    message_shapes = []
    for axis in range(3):
        message_shapes += [jax.ShapeDtypeStruct((cells // lengths[axis], k, q), BF16)] * 2
    one = 2 * k * q * q
    faces = sum(cells // n for n in lengths)
    blocks, *sends = call(
        lambda *r: prepare(lengths, *r),
        [vecs, coupling],
        [bonds],
        [jax.ShapeDtypeStruct(coupling.shape, BF16)] + message_shapes,
        faces * one,
    )
    previous = vecs
    for step in range(STEPS):
        last = step == STEPS - 1
        got = exchanged(sends)
        (total,) = call(
            lambda *r: interior(lengths, *r),
            [vecs, onsite, blocks],
            [],
            [jax.ShapeDtypeStruct((cells, k, q), F32)],
            (7 * cells - 2 * faces) * one,
        )
        result = jax.ShapeDtypeStruct((cells, k, q), F32 if last else BF16)
        following, *sends = call(
            lambda *r, step=step: finish(lengths, step, *r),
            [total, vecs, previous, blocks, *got],
            [],
            [result] if last else [result] + message_shapes,
            (faces if last else 2 * faces) * one,
        )
        previous, vecs = vecs, following
    return vecs.reshape(trial.shape)


def solution(mesh):
    placed = (
        P("gx", "gy", "gz", None, None),
        P("gx", "gy", "gz", None, None),
        P(None, "gx", "gy", "gz", None, None),
        P(None, "gx", "gy", "gz"),
    )
    return jax.shard_map(
        shards,
        mesh=mesh,
        in_specs=placed,
        out_specs=P("gx", "gy", "gz", None, None),
        check_vma=False,
    )
```

time: 159 us -> 129 us (0.81)
  the two profiles are of different devices: /device:TPU:439 before, /device:TPU:23 now
where the time goes in v1:
time: 129 us; the launch traced here: 128 us
  starting transfers between devices  95 us (74%)
  waiting for transfers between devices  20.3 us (16%)
  Pallas kernels  8.87 us (7%)
  local copies, waits for them, and re-layouts  3.11 us (2%)
    ppermute x30, starting transfers between devices, exchanged(): got.append(lax.ppermute(sends[2 * axis + which], AXES[axis], route))  95 us
    ppermute x30, waiting for transfers between devices, exchanged(): got.append(lax.ppermute(sends[2 * axis + which], AXES[axis], route))  20.3 us
    pallas_call x11, Pallas kernels, call(): pl.pallas_call(body, out_shape=shapes, in_specs=in_specs, out_specs=[pl.B...  8.87 us
    unnamed x8, local copies, waits for them, and re-layouts  3.11 us
  transfers between devices with their start and end apart: 30, of which 5 were waited for; matrix products, arithmetic and copies ran while one was open for 0% of the time, Pallas kernels for 3%

profile of v1, /device:TPU:23, one launch (start us, length us, event | category | flops | bytes accessed | tf_op | source)
XLA Modules:
  0.0 127.7 jit_solution(1192353654664739776)
XLA Ops:
  0.0 1.0 copy-done.1
  1.0 1.4 %copy-done.2 = bf16[3,2,2,4,128,128]{5,4,3,2,1,0:T(8,128)(2,1)S(1)} copy-done((bf16[3,2,2,4,128,128]{5,4,3,2,1,0:T(8,128)(2,1)S(1)}, bf16[3,2,2,4,128,128]{5,4,3,2,1,0:T(8,128)(2,1)}, u32[]{:S(2)}) %copy-start.2) | copy-done | bytes 1572888
  2.4 0.7 copy-done.3
  3.1 1.1 shard_map.46
  4.3 2.6 %collective-permute-start.4 = (bf16[4,64,128]{2,1,0:T(8,128)(2,1)S(1)}, bf16[4,64,128]{2,1,0:T(8,128)(2,1)S(1)}, u32[]{:S(2)}, u32[]{:S(2)}) collective-permute-start(bf16[4,64,128]{2,1,0:T(8,128)(2,1)S(1)} %get-tuple-element.45), channel_id=1, source_target_pairs={{0,1},{2,3},{4,5},{6,7},{8,9},{10,11},{12,13},{14,15},{16,17},{18,... | collective-permute-start | bytes 196616 | tf_op jit(solution)/shard_map/ppermute | solution.py:146
  6.8 2.0 %collective-permute-start = (bf16[8,64,128]{2,1,0:T(8,128)(2,1)S(1)}, bf16[8,64,128]{2,1,0:T(8,128)(2,1)S(1)}, u32[]{:S(2)}, u32[]{:S(2)}) collective-permute-start(bf16[8,64,128]{2,1,0:T(8,128)(2,1)S(1)} %get-tuple-element.41), channel_id=1, source_target_pairs={{0,128},{256,384},{512,640},{768,896},{128,0},{384,256},{640,512},... | collective-permute-start | bytes 393224 | tf_op jit(solution)/shard_map/ppermute | solution.py:146
  8.8 4.7 %collective-permute-start.1 = (bf16[8,64,128]{2,1,0:T(8,128)(2,1)S(1)}, bf16[8,64,128]{2,1,0:T(8,128)(2,1)S(1)}, u32[]{:S(2)}, u32[]{:S(2)}) collective-permute-start(bf16[8,64,128]{2,1,0:T(8,128)(2,1)S(1)} %get-tuple-element.42), channel_id=1, source_target_pairs={{128,256},{384,512},{640,768},{256,128},{512,384},{768,640},{129,2... | collective-permute-start | bytes 393224 | tf_op jit(solution)/shard_map/ppermute | solution.py:146
  13.5 2.1 %collective-permute-start.2 = (bf16[8,64,128]{2,1,0:T(8,128)(2,1)S(1)}, bf16[8,64,128]{2,1,0:T(8,128)(2,1)S(1)}, u32[]{:S(2)}, u32[]{:S(2)}) collective-permute-start(bf16[8,64,128]{2,1,0:T(8,128)(2,1)S(1)} %get-tuple-element.43), channel_id=1, source_target_pairs={{0,32},{64,96},{32,0},{96,64},{1,33},{65,97},{33,1},{97,65},{2,34}... | collective-permute-start | bytes 393224 | tf_op jit(solution)/shard_map/ppermute | solution.py:146
  15.6 4.5 %collective-permute-start.3 = (bf16[8,64,128]{2,1,0:T(8,128)(2,1)S(1)}, bf16[8,64,128]{2,1,0:T(8,128)(2,1)S(1)}, u32[]{:S(2)}, u32[]{:S(2)}) collective-permute-start(bf16[8,64,128]{2,1,0:T(8,128)(2,1)S(1)} %get-tuple-element.44), channel_id=1, source_target_pairs={{32,64},{64,32},{33,65},{65,33},{34,66},{66,34},{35,67},{67,35},{3... | collective-permute-start | bytes 393224 | tf_op jit(solution)/shard_map/ppermute | solution.py:146
  20.1 0.0 collective-permute-done.4.r_8_
  20.1 6.8 %collective-permute-start.5 = (bf16[4,64,128]{2,1,0:T(8,128)(2,1)S(1)}, bf16[4,64,128]{2,1,0:T(8,128)(2,1)S(1)}, u32[]{:S(2)}, u32[]{:S(2)}) collective-permute-start(bf16[4,64,128]{2,1,0:T(8,128)(2,1)S(1)} %get-tuple-element.46), channel_id=1, source_target_pairs={{1,2},{3,4},{5,6},{7,8},{9,10},{11,12},{13,14},{15,16},{17,18},{19... | collective-permute-start | bytes 196616 | tf_op jit(solution)/shard_map/ppermute | solution.py:146
  27.0 0.7 shard_map.47.r_0_
  27.7 3.5 %collective-permute-done.5.r_9_ = bf16[4,64,128]{2,1,0:T(8,128)(2,1)S(1)} collective-permute-done((bf16[4,64,128]{2,1,0:T(8,128)(2,1)S(1)}, bf16[4,64,128]{2,1,0:T(8,128)(2,1)S(1)}, u32[]{:S(2)}, u32[]{:S(2)}) %collective-permute-start.5) | collective-permute-done | bytes 65568 | tf_op jit(solution)/shard_map/ppermute | solution.py:146
  31.2 0.0 collective-permute-done.r_4_
  31.2 0.0 collective-permute-done.1.r_5_
  31.2 0.0 collective-permute-done.2.r_6_
  31.3 0.7 shard_map.48
  32.0 4.9 %collective-permute-start.10 = (bf16[4,64,128]{2,1,0:T(8,128)(2,1)S(1)}, bf16[4,64,128]{2,1,0:T(8,128)(2,1)S(1)}, u32[]{:S(2)}, u32[]{:S(2)}) collective-permute-start(bf16[4,64,128]{2,1,0:T(8,128)(2,1)S(1)} %get-tuple-element.52), channel_id=1, source_target_pairs={{0,1},{2,3},{4,5},{6,7},{8,9},{10,11},{12,13},{14,15},{16,17},{18,... | collective-permute-start | bytes 196616 | tf_op jit(solution)/shard_map/ppermute | solution.py:146
  36.9 1.9 %collective-permute-start.6 = (bf16[8,64,128]{2,1,0:T(8,128)(2,1)S(1)}, bf16[8,64,128]{2,1,0:T(8,128)(2,1)S(1)}, u32[]{:S(2)}, u32[]{:S(2)}) collective-permute-start(bf16[8,64,128]{2,1,0:T(8,128)(2,1)S(1)} %get-tuple-element.48), channel_id=1, source_target_pairs={{0,128},{256,384},{512,640},{768,896},{128,0},{384,256},{640,512},... | collective-permute-start | bytes 393224 | tf_op jit(solution)/shard_map/ppermute | solution.py:146
  38.8 3.4 %collective-permute-start.7 = (bf16[8,64,128]{2,1,0:T(8,128)(2,1)S(1)}, bf16[8,64,128]{2,1,0:T(8,128)(2,1)S(1)}, u32[]{:S(2)}, u32[]{:S(2)}) collective-permute-start(bf16[8,64,128]{2,1,0:T(8,128)(2,1)S(1)} %get-tuple-element.49), channel_id=1, source_target_pairs={{128,256},{384,512},{640,768},{256,128},{512,384},{768,640},{129,2... | collective-permute-start | bytes 393224 | tf_op jit(solution)/shard_map/ppermute | solution.py:146
  42.2 1.9 %collective-permute-start.8 = (bf16[8,64,128]{2,1,0:T(8,128)(2,1)S(1)}, bf16[8,64,128]{2,1,0:T(8,128)(2,1)S(1)}, u32[]{:S(2)}, u32[]{:S(2)}) collective-permute-start(bf16[8,64,128]{2,1,0:T(8,128)(2,1)S(1)} %get-tuple-element.50), channel_id=1, source_target_pairs={{0,32},{64,96},{32,0},{96,64},{1,33},{65,97},{33,1},{97,65},{2,34}... | collective-permute-start | bytes 393224 | tf_op jit(solution)/shard_map/ppermute | solution.py:146
  44.1 3.2 %collective-permute-start.9 = (bf16[8,64,128]{2,1,0:T(8,128)(2,1)S(1)}, bf16[8,64,128]{2,1,0:T(8,128)(2,1)S(1)}, u32[]{:S(2)}, u32[]{:S(2)}) collective-permute-start(bf16[8,64,128]{2,1,0:T(8,128)(2,1)S(1)} %get-tuple-element.51), channel_id=1, source_target_pairs={{32,64},{64,32},{33,65},{65,33},{34,66},{66,34},{35,67},{67,35},{3... | collective-permute-start | bytes 393224 | tf_op jit(solution)/shard_map/ppermute | solution.py:146
  47.3 0.0 collective-permute-done.10.r_8_
  47.3 2.9 %collective-permute-start.11 = (bf16[4,64,128]{2,1,0:T(8,128)(2,1)S(1)}, bf16[4,64,128]{2,1,0:T(8,128)(2,1)S(1)}, u32[]{:S(2)}, u32[]{:S(2)}) collective-permute-start(bf16[4,64,128]{2,1,0:T(8,128)(2,1)S(1)} %get-tuple-element.53), channel_id=1, source_target_pairs={{1,2},{3,4},{5,6},{7,8},{9,10},{11,12},{13,14},{15,16},{17,18},{19... | collective-permute-start | bytes 196616 | tf_op jit(solution)/shard_map/ppermute | solution.py:146
  50.3 0.7 shard_map.49.r_0_
  51.0 4.8 %collective-permute-done.11.r_9_ = bf16[4,64,128]{2,1,0:T(8,128)(2,1)S(1)} collective-permute-done((bf16[4,64,128]{2,1,0:T(8,128)(2,1)S(1)}, bf16[4,64,128]{2,1,0:T(8,128)(2,1)S(1)}, u32[]{:S(2)}, u32[]{:S(2)}) %collective-permute-start.11) | collective-permute-done | bytes 65568 | tf_op jit(solution)/shard_map/ppermute | solution.py:146
  55.9 0.0 collective-permute-done.6.r_4_
  55.9 0.0 collective-permute-done.7.r_5_
  55.9 0.0 collective-permute-done.8.r_6_
  55.9 0.7 shard_map.50
  56.6 3.5 %collective-permute-start.16 = (bf16[4,64,128]{2,1,0:T(8,128)(2,1)S(1)}, bf16[4,64,128]{2,1,0:T(8,128)(2,1)S(1)}, u32[]{:S(2)}, u32[]{:S(2)}) collective-permute-start(bf16[4,64,128]{2,1,0:T(8,128)(2,1)S(1)} %get-tuple-element.59), channel_id=1, source_target_pairs={{0,1},{2,3},{4,5},{6,7},{8,9},{10,11},{12,13},{14,15},{16,17},{18,... | collective-permute-start | bytes 196616 | tf_op jit(solution)/shard_map/ppermute | solution.py:146
  60.1 1.9 %collective-permute-start.12 = (bf16[8,64,128]{2,1,0:T(8,128)(2,1)S(1)}, bf16[8,64,128]{2,1,0:T(8,128)(2,1)S(1)}, u32[]{:S(2)}, u32[]{:S(2)}) collective-permute-start(bf16[8,64,128]{2,1,0:T(8,128)(2,1)S(1)} %get-tuple-element.55), channel_id=1, source_target_pairs={{0,128},{256,384},{512,640},{768,896},{128,0},{384,256},{640,512},... | collective-permute-start | bytes 393224 | tf_op jit(solution)/shard_map/ppermute | solution.py:146
  62.0 3.4 %collective-permute-start.13 = (bf16[8,64,128]{2,1,0:T(8,128)(2,1)S(1)}, bf16[8,64,128]{2,1,0:T(8,128)(2,1)S(1)}, u32[]{:S(2)}, u32[]{:S(2)}) collective-permute-start(bf16[8,64,128]{2,1,0:T(8,128)(2,1)S(1)} %get-tuple-element.56), channel_id=1, source_target_pairs={{128,256},{384,512},{640,768},{256,128},{512,384},{768,640},{129,2... | collective-permute-start | bytes 393224 | tf_op jit(solution)/shard_map/ppermute | solution.py:146
  65.4 1.9 %collective-permute-start.14 = (bf16[8,64,128]{2,1,0:T(8,128)(2,1)S(1)}, bf16[8,64,128]{2,1,0:T(8,128)(2,1)S(1)}, u32[]{:S(2)}, u32[]{:S(2)}) collective-permute-start(bf16[8,64,128]{2,1,0:T(8,128)(2,1)S(1)} %get-tuple-element.57), channel_id=1, source_target_pairs={{0,32},{64,96},{32,0},{96,64},{1,33},{65,97},{33,1},{97,65},{2,34}... | collective-permute-start | bytes 393224 | tf_op jit(solution)/shard_map/ppermute | solution.py:146
  67.3 2.0 %collective-permute-start.15 = (bf16[8,64,128]{2,1,0:T(8,128)(2,1)S(1)}, bf16[8,64,128]{2,1,0:T(8,128)(2,1)S(1)}, u32[]{:S(2)}, u32[]{:S(2)}) collective-permute-start(bf16[8,64,128]{2,1,0:T(8,128)(2,1)S(1)} %get-tuple-element.58), channel_id=1, source_target_pairs={{32,64},{64,32},{33,65},{65,33},{34,66},{66,34},{35,67},{67,35},{3... | collective-permute-start | bytes 393224 | tf_op jit(solution)/shard_map/ppermute | solution.py:146
  69.3 4.9 %collective-permute-start.17 = (bf16[4,64,128]{2,1,0:T(8,128)(2,1)S(1)}, bf16[4,64,128]{2,1,0:T(8,128)(2,1)S(1)}, u32[]{:S(2)}, u32[]{:S(2)}) collective-permute-start(bf16[4,64,128]{2,1,0:T(8,128)(2,1)S(1)} %get-tuple-element.60), channel_id=1, source_target_pairs={{1,2},{3,4},{5,6},{7,8},{9,10},{11,12},{13,14},{15,16},{17,18},{19... | collective-permute-start | bytes 196616 | tf_op jit(solution)/shard_map/ppermute | solution.py:146
  74.3 0.7 shard_map.51.r_0_
  75.0 4.4 %collective-permute-done.17.r_9_ = bf16[4,64,128]{2,1,0:T(8,128)(2,1)S(1)} collective-permute-done((bf16[4,64,128]{2,1,0:T(8,128)(2,1)S(1)}, bf16[4,64,128]{2,1,0:T(8,128)(2,1)S(1)}, u32[]{:S(2)}, u32[]{:S(2)}) %collective-permute-start.17) | collective-permute-done | bytes 65568 | tf_op jit(solution)/shard_map/ppermute | solution.py:146
  79.4 0.0 collective-permute-done.13.r_5_
  79.4 0.0 collective-permute-done.14.r_6_
  79.4 0.0 collective-permute-done.15.r_7_
  79.5 0.7 shard_map.52
  80.2 2.1 %collective-permute-start.22 = (bf16[4,64,128]{2,1,0:T(8,128)(2,1)S(1)}, bf16[4,64,128]{2,1,0:T(8,128)(2,1)S(1)}, u32[]{:S(2)}, u32[]{:S(2)}) collective-permute-start(bf16[4,64,128]{2,1,0:T(8,128)(2,1)S(1)} %get-tuple-element.66), channel_id=1, source_target_pairs={{0,1},{2,3},{4,5},{6,7},{8,9},{10,11},{12,13},{14,15},{16,17},{18,... | collective-permute-start | bytes 196616 | tf_op jit(solution)/shard_map/ppermute | solution.py:146
  82.3 1.9 %collective-permute-start.18 = (bf16[8,64,128]{2,1,0:T(8,128)(2,1)S(1)}, bf16[8,64,128]{2,1,0:T(8,128)(2,1)S(1)}, u32[]{:S(2)}, u32[]{:S(2)}) collective-permute-start(bf16[8,64,128]{2,1,0:T(8,128)(2,1)S(1)} %get-tuple-element.62), channel_id=1, source_target_pairs={{0,128},{256,384},{512,640},{768,896},{128,0},{384,256},{640,512},... | collective-permute-start | bytes 393224 | tf_op jit(solution)/shard_map/ppermute | solution.py:146
  84.2 4.7 %collective-permute-start.19 = (bf16[8,64,128]{2,1,0:T(8,128)(2,1)S(1)}, bf16[8,64,128]{2,1,0:T(8,128)(2,1)S(1)}, u32[]{:S(2)}, u32[]{:S(2)}) collective-permute-start(bf16[8,64,128]{2,1,0:T(8,128)(2,1)S(1)} %get-tuple-element.63), channel_id=1, source_target_pairs={{128,256},{384,512},{640,768},{256,128},{512,384},{768,640},{129,2... | collective-permute-start | bytes 393224 | tf_op jit(solution)/shard_map/ppermute | solution.py:146
  88.9 1.9 %collective-permute-start.20 = (bf16[8,64,128]{2,1,0:T(8,128)(2,1)S(1)}, bf16[8,64,128]{2,1,0:T(8,128)(2,1)S(1)}, u32[]{:S(2)}, u32[]{:S(2)}) collective-permute-start(bf16[8,64,128]{2,1,0:T(8,128)(2,1)S(1)} %get-tuple-element.64), channel_id=1, source_target_pairs={{0,32},{64,96},{32,0},{96,64},{1,33},{65,97},{33,1},{97,65},{2,34}... | collective-permute-start | bytes 393224 | tf_op jit(solution)/shard_map/ppermute | solution.py:146
  90.8 2.5 %collective-permute-start.21 = (bf16[8,64,128]{2,1,0:T(8,128)(2,1)S(1)}, bf16[8,64,128]{2,1,0:T(8,128)(2,1)S(1)}, u32[]{:S(2)}, u32[]{:S(2)}) collective-permute-start(bf16[8,64,128]{2,1,0:T(8,128)(2,1)S(1)} %get-tuple-element.65), channel_id=1, source_target_pairs={{32,64},{64,32},{33,65},{65,33},{34,66},{66,34},{35,67},{67,35},{3... | collective-permute-start | bytes 393224 | tf_op jit(solution)/shard_map/ppermute | solution.py:146
  93.4 0.0 collective-permute-done.22.r_8_
  93.4 5.7 %collective-permute-start.23 = (bf16[4,64,128]{2,1,0:T(8,128)(2,1)S(1)}, bf16[4,64,128]{2,1,0:T(8,128)(2,1)S(1)}, u32[]{:S(2)}, u32[]{:S(2)}) collective-permute-start(bf16[4,64,128]{2,1,0:T(8,128)(2,1)S(1)} %get-tuple-element.67), channel_id=1, source_target_pairs={{1,2},{3,4},{5,6},{7,8},{9,10},{11,12},{13,14},{15,16},{17,18},{19... | collective-permute-start | bytes 196616 | tf_op jit(solution)/shard_map/ppermute | solution.py:146
  99.0 0.7 shard_map.53.r_0_
  99.8 3.1 %collective-permute-done.23.r_9_ = bf16[4,64,128]{2,1,0:T(8,128)(2,1)S(1)} collective-permute-done((bf16[4,64,128]{2,1,0:T(8,128)(2,1)S(1)}, bf16[4,64,128]{2,1,0:T(8,128)(2,1)S(1)}, u32[]{:S(2)}, u32[]{:S(2)}) %collective-permute-start.23) | collective-permute-done | bytes 65568 | tf_op jit(solution)/shard_map/ppermute | solution.py:146
  102.9 0.0 collective-permute-done.18.r_4_
  102.9 0.0 collective-permute-done.19.r_5_
  102.9 0.0 collective-permute-done.20.r_6_
  102.9 0.7 shard_map.54
  103.6 2.7 %collective-permute-start.28 = (bf16[4,64,128]{2,1,0:T(8,128)(2,1)S(1)}, bf16[4,64,128]{2,1,0:T(8,128)(2,1)S(1)}, u32[]{:S(2)}, u32[]{:S(2)}) collective-permute-start(bf16[4,64,128]{2,1,0:T(8,128)(2,1)S(1)} %get-tuple-element.73), channel_id=1, source_target_pairs={{0,1},{2,3},{4,5},{6,7},{8,9},{10,11},{12,13},{14,15},{16,17},{18,... | collective-permute-start | bytes 196616 | tf_op jit(solution)/shard_map/ppermute | solution.py:146
  106.3 1.9 %collective-permute-start.24 = (bf16[8,64,128]{2,1,0:T(8,128)(2,1)S(1)}, bf16[8,64,128]{2,1,0:T(8,128)(2,1)S(1)}, u32[]{:S(2)}, u32[]{:S(2)}) collective-permute-start(bf16[8,64,128]{2,1,0:T(8,128)(2,1)S(1)} %get-tuple-element.69), channel_id=1, source_target_pairs={{0,128},{256,384},{512,640},{768,896},{128,0},{384,256},{640,512},... | collective-permute-start | bytes 393224 | tf_op jit(solution)/shard_map/ppermute | solution.py:146
  108.2 3.4 %collective-permute-start.25 = (bf16[8,64,128]{2,1,0:T(8,128)(2,1)S(1)}, bf16[8,64,128]{2,1,0:T(8,128)(2,1)S(1)}, u32[]{:S(2)}, u32[]{:S(2)}) collective-permute-start(bf16[8,64,128]{2,1,0:T(8,128)(2,1)S(1)} %get-tuple-element.70), channel_id=1, source_target_pairs={{128,256},{384,512},{640,768},{256,128},{512,384},{768,640},{129,2... | collective-permute-start | bytes 393224 | tf_op jit(solution)/shard_map/ppermute | solution.py:146
  111.6 1.9 %collective-permute-start.26 = (bf16[8,64,128]{2,1,0:T(8,128)(2,1)S(1)}, bf16[8,64,128]{2,1,0:T(8,128)(2,1)S(1)}, u32[]{:S(2)}, u32[]{:S(2)}) collective-permute-start(bf16[8,64,128]{2,1,0:T(8,128)(2,1)S(1)} %get-tuple-element.71), channel_id=1, source_target_pairs={{0,32},{64,96},{32,0},{96,64},{1,33},{65,97},{33,1},{97,65},{2,34}... | collective-permute-start | bytes 393224 | tf_op jit(solution)/shard_map/ppermute | solution.py:146
  113.5 2.4 %collective-permute-start.27 = (bf16[8,64,128]{2,1,0:T(8,128)(2,1)S(1)}, bf16[8,64,128]{2,1,0:T(8,128)(2,1)S(1)}, u32[]{:S(2)}, u32[]{:S(2)}) collective-permute-start(bf16[8,64,128]{2,1,0:T(8,128)(2,1)S(1)} %get-tuple-element.72), channel_id=1, source_target_pairs={{32,64},{64,32},{33,65},{65,33},{34,66},{66,34},{35,67},{67,35},{3... | collective-permute-start | bytes 393224 | tf_op jit(solution)/shard_map/ppermute | solution.py:146
  115.9 5.5 %collective-permute-start.29 = (bf16[4,64,128]{2,1,0:T(8,128)(2,1)S(1)}, bf16[4,64,128]{2,1,0:T(8,128)(2,1)S(1)}, u32[]{:S(2)}, u32[]{:S(2)}) collective-permute-start(bf16[4,64,128]{2,1,0:T(8,128)(2,1)S(1)} %get-tuple-element.74), channel_id=1, source_target_pairs={{1,2},{3,4},{5,6},{7,8},{9,10},{11,12},{13,14},{15,16},{17,18},{19... | collective-permute-start | bytes 196616 | tf_op jit(solution)/shard_map/ppermute | solution.py:146
  121.4 0.7 shard_map.55.r_0_
  122.2 4.3 %collective-permute-done.29.r_9_ = bf16[4,64,128]{2,1,0:T(8,128)(2,1)S(1)} collective-permute-done((bf16[4,64,128]{2,1,0:T(8,128)(2,1)S(1)}, bf16[4,64,128]{2,1,0:T(8,128)(2,1)S(1)}, u32[]{:S(2)}, u32[]{:S(2)}) %collective-permute-start.29) | collective-permute-done | bytes 65568 | tf_op jit(solution)/shard_map/ppermute | solution.py:146
  126.5 1.2 shard_map.56
  (15 shorter events, 0.0 us)
Async XLA Ops:
  0.0 26.9 %copy-start = (bf16[2,2,4,128,128]{4,3,2,1,0:T(8,128)(2,1)S(1)}, bf16[2,2,4,128,128]{4,3,2,1,0:T(8,128)(2,1)}, u32[]{:S(2)}) copy-start(bf16[2,2,4,128,128]{4,3,2,1,0:T(8,128)(2,1)} %param.5) | copy-start | bytes 1572868
  0.0 1.0 copy-start.1
  1.0 1.4 %copy-start.2 = (bf16[3,2,2,4,128,128]{5,4,3,2,1,0:T(8,128)(2,1)S(1)}, bf16[3,2,2,4,128,128]{5,4,3,2,1,0:T(8,128)(2,1)}, u32[]{:S(2)}) copy-start(bf16[3,2,2,4,128,128]{5,4,3,2,1,0:T(8,128)(2,1)} %param.6) | copy-start | bytes 4718596
  2.4 0.7 copy-start.3
  4.3 15.9 %collective-permute-start.4 = (bf16[4,64,128]{2,1,0:T(8,128)(2,1)S(1)}, bf16[4,64,128]{2,1,0:T(8,128)(2,1)S(1)}, u32[]{:S(2)}, u32[]{:S(2)}) collective-permute-start(bf16[4,64,128]{2,1,0:T(8,128)(2,1)S(1)} %get-tuple-element.45), channel_id=1, source_target_pairs={{0,1},{2,3},{4,5},{6,7},{8,9},{10,11},{12,13},{14,15},{16,17},{18,... | collective-permute-start | bytes 196616 | tf_op jit(solution)/shard_map/ppermute | solution.py:146
  6.8 24.4 %collective-permute-start = (bf16[8,64,128]{2,1,0:T(8,128)(2,1)S(1)}, bf16[8,64,128]{2,1,0:T(8,128)(2,1)S(1)}, u32[]{:S(2)}, u32[]{:S(2)}) collective-permute-start(bf16[8,64,128]{2,1,0:T(8,128)(2,1)S(1)} %get-tuple-element.41), channel_id=1, source_target_pairs={{0,128},{256,384},{512,640},{768,896},{128,0},{384,256},{640,512},... | collective-permute-start | bytes 393224 | tf_op jit(solution)/shard_map/ppermute | solution.py:146
  8.8 22.4 %collective-permute-start.1 = (bf16[8,64,128]{2,1,0:T(8,128)(2,1)S(1)}, bf16[8,64,128]{2,1,0:T(8,128)(2,1)S(1)}, u32[]{:S(2)}, u32[]{:S(2)}) collective-permute-start(bf16[8,64,128]{2,1,0:T(8,128)(2,1)S(1)} %get-tuple-element.42), channel_id=1, source_target_pairs={{128,256},{384,512},{640,768},{256,128},{512,384},{768,640},{129,2... | collective-permute-start | bytes 393224 | tf_op jit(solution)/shard_map/ppermute | solution.py:146
  13.5 17.7 %collective-permute-start.2 = (bf16[8,64,128]{2,1,0:T(8,128)(2,1)S(1)}, bf16[8,64,128]{2,1,0:T(8,128)(2,1)S(1)}, u32[]{:S(2)}, u32[]{:S(2)}) collective-permute-start(bf16[8,64,128]{2,1,0:T(8,128)(2,1)S(1)} %get-tuple-element.43), channel_id=1, source_target_pairs={{0,32},{64,96},{32,0},{96,64},{1,33},{65,97},{33,1},{97,65},{2,34}... | collective-permute-start | bytes 393224 | tf_op jit(solution)/shard_map/ppermute | solution.py:146
  15.6 15.6 %collective-permute-start.3 = (bf16[8,64,128]{2,1,0:T(8,128)(2,1)S(1)}, bf16[8,64,128]{2,1,0:T(8,128)(2,1)S(1)}, u32[]{:S(2)}, u32[]{:S(2)}) collective-permute-start(bf16[8,64,128]{2,1,0:T(8,128)(2,1)S(1)} %get-tuple-element.44), channel_id=1, source_target_pairs={{32,64},{64,32},{33,65},{65,33},{34,66},{66,34},{35,67},{67,35},{3... | collective-permute-start | bytes 393224 | tf_op jit(solution)/shard_map/ppermute | solution.py:146
  20.1 11.1 %collective-permute-start.5 = (bf16[4,64,128]{2,1,0:T(8,128)(2,1)S(1)}, bf16[4,64,128]{2,1,0:T(8,128)(2,1)S(1)}, u32[]{:S(2)}, u32[]{:S(2)}) collective-permute-start(bf16[4,64,128]{2,1,0:T(8,128)(2,1)S(1)} %get-tuple-element.46), channel_id=1, source_target_pairs={{1,2},{3,4},{5,6},{7,8},{9,10},{11,12},{13,14},{15,16},{17,18},{19... | collective-permute-start | bytes 196616 | tf_op jit(solution)/shard_map/ppermute | solution.py:146
  32.0 15.4 %collective-permute-start.10 = (bf16[4,64,128]{2,1,0:T(8,128)(2,1)S(1)}, bf16[4,64,128]{2,1,0:T(8,128)(2,1)S(1)}, u32[]{:S(2)}, u32[]{:S(2)}) collective-permute-start(bf16[4,64,128]{2,1,0:T(8,128)(2,1)S(1)} %get-tuple-element.52), channel_id=1, source_target_pairs={{0,1},{2,3},{4,5},{6,7},{8,9},{10,11},{12,13},{14,15},{16,17},{18,... | collective-permute-start | bytes 196616 | tf_op jit(solution)/shard_map/ppermute | solution.py:146
  36.9 19.0 %collective-permute-start.6 = (bf16[8,64,128]{2,1,0:T(8,128)(2,1)S(1)}, bf16[8,64,128]{2,1,0:T(8,128)(2,1)S(1)}, u32[]{:S(2)}, u32[]{:S(2)}) collective-permute-start(bf16[8,64,128]{2,1,0:T(8,128)(2,1)S(1)} %get-tuple-element.48), channel_id=1, source_target_pairs={{0,128},{256,384},{512,640},{768,896},{128,0},{384,256},{640,512},... | collective-permute-start | bytes 393224 | tf_op jit(solution)/shard_map/ppermute | solution.py:146
  38.8 17.1 %collective-permute-start.7 = (bf16[8,64,128]{2,1,0:T(8,128)(2,1)S(1)}, bf16[8,64,128]{2,1,0:T(8,128)(2,1)S(1)}, u32[]{:S(2)}, u32[]{:S(2)}) collective-permute-start(bf16[8,64,128]{2,1,0:T(8,128)(2,1)S(1)} %get-tuple-element.49), channel_id=1, source_target_pairs={{128,256},{384,512},{640,768},{256,128},{512,384},{768,640},{129,2... | collective-permute-start | bytes 393224 | tf_op jit(solution)/shard_map/ppermute | solution.py:146
  42.2 13.7 %collective-permute-start.8 = (bf16[8,64,128]{2,1,0:T(8,128)(2,1)S(1)}, bf16[8,64,128]{2,1,0:T(8,128)(2,1)S(1)}, u32[]{:S(2)}, u32[]{:S(2)}) collective-permute-start(bf16[8,64,128]{2,1,0:T(8,128)(2,1)S(1)} %get-tuple-element.50), channel_id=1, source_target_pairs={{0,32},{64,96},{32,0},{96,64},{1,33},{65,97},{33,1},{97,65},{2,34}... | collective-permute-start | bytes 393224 | tf_op jit(solution)/shard_map/ppermute | solution.py:146
  44.1 11.8 %collective-permute-start.9 = (bf16[8,64,128]{2,1,0:T(8,128)(2,1)S(1)}, bf16[8,64,128]{2,1,0:T(8,128)(2,1)S(1)}, u32[]{:S(2)}, u32[]{:S(2)}) collective-permute-start(bf16[8,64,128]{2,1,0:T(8,128)(2,1)S(1)} %get-tuple-element.51), channel_id=1, source_target_pairs={{32,64},{64,32},{33,65},{65,33},{34,66},{66,34},{35,67},{67,35},{3... | collective-permute-start | bytes 393224 | tf_op jit(solution)/shard_map/ppermute | solution.py:146
  47.3 8.5 %collective-permute-start.11 = (bf16[4,64,128]{2,1,0:T(8,128)(2,1)S(1)}, bf16[4,64,128]{2,1,0:T(8,128)(2,1)S(1)}, u32[]{:S(2)}, u32[]{:S(2)}) collective-permute-start(bf16[4,64,128]{2,1,0:T(8,128)(2,1)S(1)} %get-tuple-element.53), channel_id=1, source_target_pairs={{1,2},{3,4},{5,6},{7,8},{9,10},{11,12},{13,14},{15,16},{17,18},{19... | collective-permute-start | bytes 196616 | tf_op jit(solution)/shard_map/ppermute | solution.py:146
  56.6 12.7 %collective-permute-start.16 = (bf16[4,64,128]{2,1,0:T(8,128)(2,1)S(1)}, bf16[4,64,128]{2,1,0:T(8,128)(2,1)S(1)}, u32[]{:S(2)}, u32[]{:S(2)}) collective-permute-start(bf16[4,64,128]{2,1,0:T(8,128)(2,1)S(1)} %get-tuple-element.59), channel_id=1, source_target_pairs={{0,1},{2,3},{4,5},{6,7},{8,9},{10,11},{12,13},{14,15},{16,17},{18,... | collective-permute-start | bytes 196616 | tf_op jit(solution)/shard_map/ppermute | solution.py:146
  60.1 19.3 %collective-permute-start.12 = (bf16[8,64,128]{2,1,0:T(8,128)(2,1)S(1)}, bf16[8,64,128]{2,1,0:T(8,128)(2,1)S(1)}, u32[]{:S(2)}, u32[]{:S(2)}) collective-permute-start(bf16[8,64,128]{2,1,0:T(8,128)(2,1)S(1)} %get-tuple-element.55), channel_id=1, source_target_pairs={{0,128},{256,384},{512,640},{768,896},{128,0},{384,256},{640,512},... | collective-permute-start | bytes 393224 | tf_op jit(solution)/shard_map/ppermute | solution.py:146
  62.0 17.4 %collective-permute-start.13 = (bf16[8,64,128]{2,1,0:T(8,128)(2,1)S(1)}, bf16[8,64,128]{2,1,0:T(8,128)(2,1)S(1)}, u32[]{:S(2)}, u32[]{:S(2)}) collective-permute-start(bf16[8,64,128]{2,1,0:T(8,128)(2,1)S(1)} %get-tuple-element.56), channel_id=1, source_target_pairs={{128,256},{384,512},{640,768},{256,128},{512,384},{768,640},{129,2... | collective-permute-start | bytes 393224 | tf_op jit(solution)/shard_map/ppermute | solution.py:146
  65.4 14.0 %collective-permute-start.14 = (bf16[8,64,128]{2,1,0:T(8,128)(2,1)S(1)}, bf16[8,64,128]{2,1,0:T(8,128)(2,1)S(1)}, u32[]{:S(2)}, u32[]{:S(2)}) collective-permute-start(bf16[8,64,128]{2,1,0:T(8,128)(2,1)S(1)} %get-tuple-element.57), channel_id=1, source_target_pairs={{0,32},{64,96},{32,0},{96,64},{1,33},{65,97},{33,1},{97,65},{2,34}... | collective-permute-start | bytes 393224 | tf_op jit(solution)/shard_map/ppermute | solution.py:146
  67.3 12.1 %collective-permute-start.15 = (bf16[8,64,128]{2,1,0:T(8,128)(2,1)S(1)}, bf16[8,64,128]{2,1,0:T(8,128)(2,1)S(1)}, u32[]{:S(2)}, u32[]{:S(2)}) collective-permute-start(bf16[8,64,128]{2,1,0:T(8,128)(2,1)S(1)} %get-tuple-element.58), channel_id=1, source_target_pairs={{32,64},{64,32},{33,65},{65,33},{34,66},{66,34},{35,67},{67,35},{3... | collective-permute-start | bytes 393224 | tf_op jit(solution)/shard_map/ppermute | solution.py:146
  69.3 10.1 %collective-permute-start.17 = (bf16[4,64,128]{2,1,0:T(8,128)(2,1)S(1)}, bf16[4,64,128]{2,1,0:T(8,128)(2,1)S(1)}, u32[]{:S(2)}, u32[]{:S(2)}) collective-permute-start(bf16[4,64,128]{2,1,0:T(8,128)(2,1)S(1)} %get-tuple-element.60), channel_id=1, source_target_pairs={{1,2},{3,4},{5,6},{7,8},{9,10},{11,12},{13,14},{15,16},{17,18},{19... | collective-permute-start | bytes 196616 | tf_op jit(solution)/shard_map/ppermute | solution.py:146
  80.2 13.2 %collective-permute-start.22 = (bf16[4,64,128]{2,1,0:T(8,128)(2,1)S(1)}, bf16[4,64,128]{2,1,0:T(8,128)(2,1)S(1)}, u32[]{:S(2)}, u32[]{:S(2)}) collective-permute-start(bf16[4,64,128]{2,1,0:T(8,128)(2,1)S(1)} %get-tuple-element.66), channel_id=1, source_target_pairs={{0,1},{2,3},{4,5},{6,7},{8,9},{10,11},{12,13},{14,15},{16,17},{18,... | collective-permute-start | bytes 196616 | tf_op jit(solution)/shard_map/ppermute | solution.py:146
  82.3 20.6 %collective-permute-start.18 = (bf16[8,64,128]{2,1,0:T(8,128)(2,1)S(1)}, bf16[8,64,128]{2,1,0:T(8,128)(2,1)S(1)}, u32[]{:S(2)}, u32[]{:S(2)}) collective-permute-start(bf16[8,64,128]{2,1,0:T(8,128)(2,1)S(1)} %get-tuple-element.62), channel_id=1, source_target_pairs={{0,128},{256,384},{512,640},{768,896},{128,0},{384,256},{640,512},... | collective-permute-start | bytes 393224 | tf_op jit(solution)/shard_map/ppermute | solution.py:146
  84.2 18.7 %collective-permute-start.19 = (bf16[8,64,128]{2,1,0:T(8,128)(2,1)S(1)}, bf16[8,64,128]{2,1,0:T(8,128)(2,1)S(1)}, u32[]{:S(2)}, u32[]{:S(2)}) collective-permute-start(bf16[8,64,128]{2,1,0:T(8,128)(2,1)S(1)} %get-tuple-element.63), channel_id=1, source_target_pairs={{128,256},{384,512},{640,768},{256,128},{512,384},{768,640},{129,2... | collective-permute-start | bytes 393224 | tf_op jit(solution)/shard_map/ppermute | solution.py:146
  88.9 14.0 %collective-permute-start.20 = (bf16[8,64,128]{2,1,0:T(8,128)(2,1)S(1)}, bf16[8,64,128]{2,1,0:T(8,128)(2,1)S(1)}, u32[]{:S(2)}, u32[]{:S(2)}) collective-permute-start(bf16[8,64,128]{2,1,0:T(8,128)(2,1)S(1)} %get-tuple-element.64), channel_id=1, source_target_pairs={{0,32},{64,96},{32,0},{96,64},{1,33},{65,97},{33,1},{97,65},{2,34}... | collective-permute-start | bytes 393224 | tf_op jit(solution)/shard_map/ppermute | solution.py:146
  90.8 12.1 %collective-permute-start.21 = (bf16[8,64,128]{2,1,0:T(8,128)(2,1)S(1)}, bf16[8,64,128]{2,1,0:T(8,128)(2,1)S(1)}, u32[]{:S(2)}, u32[]{:S(2)}) collective-permute-start(bf16[8,64,128]{2,1,0:T(8,128)(2,1)S(1)} %get-tuple-element.65), channel_id=1, source_target_pairs={{32,64},{64,32},{33,65},{65,33},{34,66},{66,34},{35,67},{67,35},{3... | collective-permute-start | bytes 393224 | tf_op jit(solution)/shard_map/ppermute | solution.py:146
  93.4 9.5 %collective-permute-start.23 = (bf16[4,64,128]{2,1,0:T(8,128)(2,1)S(1)}, bf16[4,64,128]{2,1,0:T(8,128)(2,1)S(1)}, u32[]{:S(2)}, u32[]{:S(2)}) collective-permute-start(bf16[4,64,128]{2,1,0:T(8,128)(2,1)S(1)} %get-tuple-element.67), channel_id=1, source_target_pairs={{1,2},{3,4},{5,6},{7,8},{9,10},{11,12},{13,14},{15,16},{17,18},{19... | collective-permute-start | bytes 196616 | tf_op jit(solution)/shard_map/ppermute | solution.py:146
  103.6 12.3 %collective-permute-start.28 = (bf16[4,64,128]{2,1,0:T(8,128)(2,1)S(1)}, bf16[4,64,128]{2,1,0:T(8,128)(2,1)S(1)}, u32[]{:S(2)}, u32[]{:S(2)}) collective-permute-start(bf16[4,64,128]{2,1,0:T(8,128)(2,1)S(1)} %get-tuple-element.73), channel_id=1, source_target_pairs={{0,1},{2,3},{4,5},{6,7},{8,9},{10,11},{12,13},{14,15},{16,17},{18,... | collective-permute-start | bytes 196616 | tf_op jit(solution)/shard_map/ppermute | solution.py:146
  106.3 20.2 %collective-permute-start.24 = (bf16[8,64,128]{2,1,0:T(8,128)(2,1)S(1)}, bf16[8,64,128]{2,1,0:T(8,128)(2,1)S(1)}, u32[]{:S(2)}, u32[]{:S(2)}) collective-permute-start(bf16[8,64,128]{2,1,0:T(8,128)(2,1)S(1)} %get-tuple-element.69), channel_id=1, source_target_pairs={{0,128},{256,384},{512,640},{768,896},{128,0},{384,256},{640,512},... | collective-permute-start | bytes 393224 | tf_op jit(solution)/shard_map/ppermute | solution.py:146
  108.2 18.2 %collective-permute-start.25 = (bf16[8,64,128]{2,1,0:T(8,128)(2,1)S(1)}, bf16[8,64,128]{2,1,0:T(8,128)(2,1)S(1)}, u32[]{:S(2)}, u32[]{:S(2)}) collective-permute-start(bf16[8,64,128]{2,1,0:T(8,128)(2,1)S(1)} %get-tuple-element.70), channel_id=1, source_target_pairs={{128,256},{384,512},{640,768},{256,128},{512,384},{768,640},{129,2... | collective-permute-start | bytes 393224 | tf_op jit(solution)/shard_map/ppermute | solution.py:146
  111.6 14.9 %collective-permute-start.26 = (bf16[8,64,128]{2,1,0:T(8,128)(2,1)S(1)}, bf16[8,64,128]{2,1,0:T(8,128)(2,1)S(1)}, u32[]{:S(2)}, u32[]{:S(2)}) collective-permute-start(bf16[8,64,128]{2,1,0:T(8,128)(2,1)S(1)} %get-tuple-element.71), channel_id=1, source_target_pairs={{0,32},{64,96},{32,0},{96,64},{1,33},{65,97},{33,1},{97,65},{2,34}... | collective-permute-start | bytes 393224 | tf_op jit(solution)/shard_map/ppermute | solution.py:146
  113.5 13.0 %collective-permute-start.27 = (bf16[8,64,128]{2,1,0:T(8,128)(2,1)S(1)}, bf16[8,64,128]{2,1,0:T(8,128)(2,1)S(1)}, u32[]{:S(2)}, u32[]{:S(2)}) collective-permute-start(bf16[8,64,128]{2,1,0:T(8,128)(2,1)S(1)} %get-tuple-element.72), channel_id=1, source_target_pairs={{32,64},{64,32},{33,65},{65,33},{34,66},{66,34},{35,67},{67,35},{3... | collective-permute-start | bytes 393224 | tf_op jit(solution)/shard_map/ppermute | solution.py:146
  115.9 10.5 %collective-permute-start.29 = (bf16[4,64,128]{2,1,0:T(8,128)(2,1)S(1)}, bf16[4,64,128]{2,1,0:T(8,128)(2,1)S(1)}, u32[]{:S(2)}, u32[]{:S(2)}) collective-permute-start(bf16[4,64,128]{2,1,0:T(8,128)(2,1)S(1)} %get-tuple-element.74), channel_id=1, source_target_pairs={{1,2},{3,4},{5,6},{7,8},{9,10},{11,12},{13,14},{15,16},{17,18},{19... | collective-permute-start | bytes 196616 | tf_op jit(solution)/shard_map/ppermute | solution.py:146
